TPU v7x, 128 devices: a whole 4x4x4 slice. The times are simulated.
128 devices in a mesh: dx: 8 (over z, core), dy: 16 (over x, y).
Axes of the slice: x: 4, y: 4, z: 4, core: 2. Of those that a mesh axis runs over, the one named last changes fastest.
Arguments:
- orbitals: bfloat16 [112, 224, 13, 256], P('dx', 'dy'), may hold values from -6 to 6
- elem_mats: bfloat16 [16, 32, 2, 512, 512], P('dx', 'dy'), as said below
- conn: int32 [16, 32, 2, 512], P('dx', 'dy'), may hold values from 0 to 3374, as said below
Outputs:
- filtered: float32 [112, 224, 13, 256], P('dx', 'dy')
Inputs may be any that keep to these rules, and one draw needn't show every extreme that they name: conn[e1, e2, e3, k] is ((7 (e1 mod 2) + a) (15) + 7 (e2 mod 2) + b) * 15 + 7 e3 + c for a node (a, b, c) of the element, 0 <= a, b, c <= 7, and each of the element's 512 nodes appears exactly once. `elem_mats`: each element's matrix is symmetric.
All inputs are finite; a program needn't handle non-finite values.
Results may differ from a plain program's by a relative error of at most 0.0059.
Values may be sent and summed in bfloat16 or wider, within the bound.
A program may use at most 128 MiB of HBM per device.

v0:
```python
import math

import jax
import jax.numpy as jnp
from jax import lax
from jax.sharding import PartitionSpec as P

filter_center = 1.5
filter_half = 4.0


def shifted(block, axis, distance):
    devices = range(lax.axis_size(axis))
    route = [(i - distance, i) for i in devices if i - distance in devices]
    return lax.ppermute(block, axis, route)


def apply_operator(field, elem_mats, conn):
    bands = field.shape[3]
    padded = jnp.pad(field, ((0, 0), (0, 0), (1, 1), (0, 0)))
    lower_plane = shifted(padded[-1], "dx", 1)
    extended = jnp.concatenate([lower_plane[None], padded], axis=0)
    side_plane = shifted(extended[:, -1], "dy", 1)
    extended = jnp.concatenate([side_plane[:, None], extended], axis=1)
    width = extended.shape[0]
    depth = extended.shape[2]
    flat = extended.reshape(-1, bands)
    nodes = elem_mats.shape[-1]
    count = elem_mats.shape[0] * elem_mats.shape[1] * elem_mats.shape[2]
    links = conn.reshape(-1)
    rows = jnp.take(flat, links, axis=0).reshape(count, nodes, bands)
    product = jnp.einsum(
        "eij,ejb->eib",
        elem_mats.reshape(count, nodes, nodes),
        rows,
        preferred_element_type=jnp.float32,
    )
    summed = (
        jnp.zeros((flat.shape[0], bands), jnp.float32).at[links].add(product.reshape(-1, bands))
    )
    summed = summed.reshape(width, width, depth, bands)
    back_y = shifted(summed[:, 0], "dy", -1)
    summed = summed[:, 1:].at[:, -1].add(back_y)
    back_x = shifted(summed[0], "dx", -1)
    summed = summed[1:].at[-1].add(back_x)
    return summed[:, :, 1:-1]


def gram_of(left, right):
    return jnp.einsum("rb,rc->bc", left, right, precision=lax.Precision.HIGHEST)


def shards(orbitals, elem_mats, conn):
    previous = orbitals.astype(jnp.float32)
    image = apply_operator(orbitals, elem_mats, conn)
    current = (image - filter_center * previous) / filter_half
    for turn in range(2):
        field = current.astype(jnp.bfloat16)
        image = apply_operator(field, elem_mats, conn)
        following = 2.0 * (image - filter_center * current) / filter_half - previous
        previous, current = (current, following)
    bands = current.shape[3]
    columns = current.reshape(-1, bands)
    gram_local = gram_of(columns, columns)
    gram_total = lax.psum(gram_local, ("dx", "dy"))
    lower = jnp.linalg.cholesky(gram_total)
    identity = jnp.eye(bands, dtype=jnp.float32)
    inverse_lower = lax.linalg.triangular_solve(lower, identity, left_side=True, lower=True)
    basis = jnp.einsum("rb,cb->rc", columns, inverse_lower, precision=lax.Precision.HIGHEST)
    scale = math.sqrt(columns.shape[0] * lax.axis_size(("dx", "dy")))
    return (basis * scale).reshape(current.shape)


def solution(mesh):
    in_specs = (
        P("dx", "dy", None, None),
        P("dx", "dy", None, None, None),
        P("dx", "dy", None, None),
    )
    out_specs = P("dx", "dy", None, None)
    return jax.shard_map(shards, mesh=mesh, in_specs=in_specs, out_specs=out_specs, check_vma=False)
```

profile of v0, /device:TPU:1, one launch (start us, length us, event | category | flops | bytes accessed | tf_op | source)
XLA Modules:
  0.0 521.1 jit_solution(5483834711174866498)
XLA Ops:
  8.5 4.9 collective-permute-start
  15.2 3.2 collective-permute-start.1
  21.9 2.6 reshape.312
  24.5 17.0 %gather_fusion = bf16[4096,256]{1,0:T(8,128)(2,1)} fusion(bf16[3375,256]{1,0:T(8,128)(2,1)S(1)} %reshape.312, s32[4096]{0:T(1024)S(1)} %fusion.33), kind=kCustom, calls=%fused_computation.clone | custom fusion | bytes 4210688 | tf_op jit(solution)/shard_map/jit(_take)/gather | solution.py:31
  41.5 2.1 broadcast_select_fusion
  44.3 3.3 convolution_bitcast_fusion.2
  47.6 5.4 %copy.26 = f32[8,512,256]{2,1,0:T(8,128)} copy(f32[8,512,256]{1,2,0:T(8,128)} %convolution_bitcast_fusion.2) | data formatting | bytes 8388608 | tf_op jit(solution)/shard_map/eij,ejb->eib/dot_general | solution.py:32
  53.0 23.7 %scatter_custom_fusion = f32[3375,256]{1,0:T(8,128)S(1)} fusion(s32[4096]{0:T(1024)S(1)} %bitcast.143, f32[4096,256]{1,0:T(8,128)} %bitcast.129, f32[]{:T(128)} %constant.229.clone.1), kind=kCustom, calls=%fused_computation.31 | custom fusion | flops 1048576 | bytes 3456512 | tf_op jit(solution)/shard_map/scatter-add | solution.py:39
  76.7 2.2 reshape.317
  81.6 7.5 %collective-permute-done.2 = f32[15,15,256]{2,1,0:T(8,128)S(1)} collective-permute-done((f32[15,15,256]{2,1,0:T(8,128)S(1)}, f32[15,15,256]{2,1,0:T(8,128)S(1)}, u32[]{:S(2)}, u32[]{:S(2)}) %collective-permute-start.2) | collective-permute-done | bytes 230432 | tf_op jit(solution)/shard_map/ppermute | solution.py:15
  91.6 6.7 %collective-permute-done.3 = f32[14,15,256]{2,1,0:T(8,128)S(1)} collective-permute-done((f32[14,15,256]{2,1,0:T(8,128)S(1)}, f32[14,15,256]{2,1,0:T(8,128)S(1)}, u32[]{:S(2)}, u32[]{:S(2)}) %collective-permute-start.3) | collective-permute-done | bytes 215072 | tf_op jit(solution)/shard_map/ppermute | solution.py:15
  103.8 3.8 collective-permute-start.5
  107.6 2.5 collective-permute-done.5
  111.7 2.6 reshape.320
  114.2 17.0 %gather_fusion.1 = bf16[4096,256]{1,0:T(8,128)(2,1)} fusion(bf16[3375,256]{1,0:T(8,128)(2,1)S(1)} %reshape.320, s32[4096]{0:T(1024)S(1)} %fusion.33), kind=kCustom, calls=%fused_computation.1.clone | custom fusion | bytes 4210688 | tf_op jit(solution)/shard_map/jit(_take)/gather | solution.py:31
  131.3 2.1 broadcast_select_fusion.1
  134.1 3.3 convolution_bitcast_fusion.1
  137.4 5.4 %copy.32 = f32[8,512,256]{2,1,0:T(8,128)} copy(f32[8,512,256]{1,2,0:T(8,128)} %convolution_bitcast_fusion.1) | data formatting | bytes 8388608 | tf_op jit(solution)/shard_map/eij,ejb->eib/dot_general | solution.py:32
  142.8 24.8 %scatter_custom_fusion.1 = f32[3375,256]{1,0:T(8,128)} fusion(s32[4096]{0:T(1024)S(1)} %bitcast.144, f32[4096,256]{1,0:T(8,128)} %bitcast.130, f32[]{:T(128)} %constant.229.clone.1), kind=kCustom, calls=%fused_computation.29 | custom fusion | flops 1048576 | bytes 3456512 | tf_op jit(solution)/shard_map/scatter-add | solution.py:39
  167.6 4.7 reshape.323
  175.0 8.6 %collective-permute-done.6 = f32[15,15,256]{2,1,0:T(8,128)S(1)} collective-permute-done((f32[15,15,256]{2,1,0:T(8,128)S(1)}, f32[15,15,256]{2,1,0:T(8,128)S(1)}, u32[]{:S(2)}, u32[]{:S(2)}) %collective-permute-start.6) | collective-permute-done | bytes 230432 | tf_op jit(solution)/shard_map/ppermute | solution.py:15
  183.7 3.3 collective-permute-start.7
  187.3 4.0 collective-permute-done.7
  196.9 4.3 collective-permute-start.9
  201.2 2.8 collective-permute-done.9
  205.5 2.6 reshape.326
  208.1 17.0 %gather_fusion.2 = bf16[4096,256]{1,0:T(8,128)(2,1)} fusion(bf16[3375,256]{1,0:T(8,128)(2,1)S(1)} %reshape.326, s32[4096]{0:T(1024)S(1)} %fusion.33), kind=kCustom, calls=%fused_computation.2.clone | custom fusion | bytes 4210688 | tf_op jit(solution)/shard_map/jit(_take)/gather | solution.py:31
  225.1 2.1 broadcast_select_fusion.2
  227.9 3.3 convolution_bitcast_fusion
  231.2 5.4 %copy.36 = f32[8,512,256]{2,1,0:T(8,128)} copy(f32[8,512,256]{1,2,0:T(8,128)} %convolution_bitcast_fusion) | data formatting | bytes 8388608 | tf_op jit(solution)/shard_map/eij,ejb->eib/dot_general | solution.py:32
  236.6 23.7 %scatter_custom_fusion.2 = f32[3375,256]{1,0:T(8,128)S(1)} fusion(s32[4096]{0:T(1024)S(1)} %bitcast.145, f32[4096,256]{1,0:T(8,128)} %bitcast.128, f32[]{:T(128)} %constant.229.clone.1), kind=kCustom, calls=%fused_computation.27 | custom fusion | flops 1048576 | bytes 3456512 | tf_op jit(solution)/shard_map/scatter-add | solution.py:39
  260.3 2.2 reshape.329
  265.2 8.6 %collective-permute-done.10 = f32[15,15,256]{2,1,0:T(8,128)S(1)} collective-permute-done((f32[15,15,256]{2,1,0:T(8,128)S(1)}, f32[15,15,256]{2,1,0:T(8,128)S(1)}, u32[]{:S(2)}, u32[]{:S(2)}) %collective-permute-start.10) | collective-permute-done | bytes 230432 | tf_op jit(solution)/shard_map/ppermute | solution.py:15
  273.9 3.3 collective-permute-start.11
  277.6 3.9 collective-permute-done.11
  281.6 2.4 fusion.2
  284.0 6.0 %convolution_bitcast_fusion.3 = f32[256,256]{0,1:T(8,128)} fusion(f32[14,14,13,256]{3,2,1,0:T(8,128)S(1)} %fusion.2), kind=kOutput, calls=%fused_computation.34 | convolution fusion | flops 2003828736 | bytes 2871296 | tf_op jit(solution)/shard_map/rb,rc->bc/dot_general | solution.py:50
  291.9 147.0 %all-reduce.6.cloned.1.call-done = f32[256,256]{0,1:T(8,128)} async-done(((f32[256,256]{0,1:T(8,128)}), f32[256,256]{0,1:T(8,128)}) %all-reduce.6.cloned.1.call-update) | async-done | bytes 262160 | tf_op jit(solution)/shard_map/psum | solution.py:65
  440.9 11.7 %cholesky.50 = f32[128,128]{1,0:T(8,128)S(1)} custom-call(f32[128,128]{1,0:T(8,128)S(1)} %cholesky.118), custom_call_target="Cholesky" | custom-call | tf_op jit(solution)/shard_map/jit(cholesky)/cholesky | solution.py:66
  452.7 10.0 %custom-call.14 = f32[1,128,128]{1,2,0:T(8,128)S(1)} custom-call(f32[1,128,128]{2,1,0:T(8,128)S(1)} %get-tuple-element.99), custom_call_target="InvertDiagBlocksLowerTriangular" | custom-call | tf_op jit(solution)/shard_map/jit(cholesky)/cholesky | solution.py:66
  463.2 11.7 %cholesky.105 = f32[128,128]{1,0:T(8,128)S(1)} custom-call(f32[128,128]{1,0:T(8,128)S(1)} %convolution_subtract_fusion.1), custom_call_target="Cholesky" | custom-call | tf_op jit(solution)/shard_map/jit(cholesky)/cholesky | solution.py:66
  477.2 5.5 %while.7 = (s32[]{:T(128)}, f32[256,256]{1,0:T(8,128)S(1)}, s32[2,2]{1,0:T(2,128)S(1)}, f32[2,128,128]{2,1,0:T(8,128)}, s32[]{:T(128)}) while((s32[]{:T(128)}, f32[256,256]{1,0:T(8,128)S(1)}, s32[2,2]{1,0:T(2,128)S(1)}, f32[2,128,128]{2,1,0:T(8,128)}, s32[]{:T(128)}) %tuple.48), condition=%wide.while_cond.6, body=%wide.while_body.6.sunk | while | flops 2 | bytes 132705 | solution.py:68
  477.9 2.1 bitcast_dynamic-update-slice_fusion.2
  480.6 2.1 bitcast_dynamic-update-slice_fusion.2
  482.7 20.5 %custom-call.15 = f32[2,128,128]{1,2,0:T(8,128)S(1)} custom-call(f32[2,128,128]{2,1,0:T(8,128)} %get-tuple-element.85), custom_call_target="InvertDiagBlocksLowerTriangular" | custom-call | tf_op jit(solution)/shard_map/triangular_solve | solution.py:68
  504.1 3.7 convolution_multiply_fusion
  507.8 2.6 reshape.333
  510.4 3.5 copy.42
  (106 shorter events, 42.1 us)
Async XLA Ops:
  6.5 6.9 %copy-start.14 = (s32[2,2,2,512]{3,2,1,0:T(2,128)S(1)}, s32[2,2,2,512]{3,2,1,0:T(2,128)}, u32[]{:S(2)}) copy-start(s32[2,2,2,512]{3,2,1,0:T(2,128)} %param.19) | copy-start | bytes 49156
  6.5 432.3 %all-reduce.6.cloned.1.call-start = ((), (), s32[]{:S(2)}) async-start(), calls=%async_computation | async-start | bytes 524288 | tf_op jit(solution)/shard_map/psum | solution.py:65
  8.5 6.7 %collective-permute-start = (bf16[14,15,256]{2,1,0:T(8,128)(2,1)S(1)}, bf16[14,15,256]{2,1,0:T(8,128)(2,1)S(1)}, u32[]{:S(2)}, u32[]{:S(2)}) collective-permute-start(bf16[14,15,256]{2,1,0:T(8,128)(2,1)S(1)} %slice_bitcast_fusion.9), channel_id=1, source_target_pairs={{0,16},{16,32},{32,48},{48,64},{64,80},{80,96},{96,112},{1,17},{17... | collective-permute-start | bytes 322568 | tf_op jit(solution)/shard_map/ppermute | solution.py:15
  15.2 5.1 collective-permute-start.1
  41.5 2.8 copy-start.3
  78.9 10.2 %copy-start.10 = (f32[15,15,15,256]{3,2,1,0:T(8,128)S(1)}, f32[15,15,15,256]{3,2,1,0:T(8,128)}, u32[]{:S(2)}) copy-start(f32[15,15,15,256]{3,2,1,0:T(8,128)} %reshape.317) | copy-start | bytes 10368004
  80.0 9.1 %slice-start = ((f32[15,15,15,256]{3,2,1,0:T(8,128)}), f32[15,14,15,256]{3,2,1,0:T(8,128)S(1)}, s32[]{:S(2)}) async-start(f32[15,15,15,256]{3,2,1,0:T(8,128)} %reshape.317), calls=%async_computation.1 | async-start | bytes 6881280 | tf_op jit(solution)/shard_map/slice | solution.py:43
  80.1 9.1 %collective-permute-start.2 = (f32[15,15,256]{2,1,0:T(8,128)S(1)}, f32[15,15,256]{2,1,0:T(8,128)S(1)}, u32[]{:S(2)}, u32[]{:S(2)}) collective-permute-start(f32[15,15,256]{2,1,0:T(8,128)S(1)} %slice_bitcast_fusion.2), channel_id=1, source_target_pairs={{1,0},{2,1},{3,2},{4,3},{5,4},{6,5},{7,6},{8,7},{9,8},{10,9},{11,1... | collective-permute-start | bytes 691208 | tf_op jit(solution)/shard_map/ppermute | solution.py:15
  89.2 9.2 %copy-start.8 = (bf16[14,14,13,256]{3,1,2,0:T(8,128)(2,1)S(1)}, bf16[14,14,13,256]{3,1,2,0:T(8,128)(2,1)}, u32[]{:S(2)}) copy-start(bf16[14,14,13,256]{3,1,2,0:T(8,128)(2,1)} %param.17) | copy-start | bytes 3913732
  89.2 9.1 %collective-permute-start.3 = (f32[14,15,256]{2,1,0:T(8,128)S(1)}, f32[14,15,256]{2,1,0:T(8,128)S(1)}, u32[]{:S(2)}, u32[]{:S(2)}) collective-permute-start(f32[14,15,256]{2,1,0:T(8,128)S(1)} %slice_bitcast_fusion.6), channel_id=1, source_target_pairs={{16,0},{32,16},{48,32},{64,48},{80,64},{96,80},{112,96},{17,1},{33... | collective-permute-start | bytes 645128 | tf_op jit(solution)/shard_map/ppermute | solution.py:15
  98.4 1.7 copy-start
  100.1 3.7 collective-permute-start.4
  103.8 6.4 %collective-permute-start.5 = (bf16[15,15,256]{2,1,0:T(8,128)(2,1)S(1)}, bf16[15,15,256]{2,1,0:T(8,128)(2,1)S(1)}, u32[]{:S(2)}, u32[]{:S(2)}) collective-permute-start(bf16[15,15,256]{2,1,0:T(8,128)(2,1)S(1)} %fusion.26), channel_id=1, source_target_pairs={{0,1},{1,2},{2,3},{3,4},{4,5},{5,6},{6,7},{7,8},{8,9},{9,10},{10,1... | collective-permute-start | bytes 345608 | tf_op jit(solution)/shard_map/ppermute | solution.py:15
  131.3 2.8 copy-start.4
  172.3 11.3 %copy-start.11 = (f32[15,15,15,256]{3,2,1,0:T(8,128)S(1)}, f32[15,15,15,256]{3,2,1,0:T(8,128)}, u32[]{:S(2)}) copy-start(f32[15,15,15,256]{3,2,1,0:T(8,128)} %reshape.323) | copy-start | bytes 10368004
  173.4 10.2 %slice-start.1 = ((f32[15,15,15,256]{3,2,1,0:T(8,128)}), f32[15,14,15,256]{3,2,1,0:T(8,128)S(1)}, s32[]{:S(2)}) async-start(f32[15,15,15,256]{3,2,1,0:T(8,128)} %reshape.323), calls=%async_computation.2 | async-start | bytes 6881280 | tf_op jit(solution)/shard_map/slice | solution.py:43
  173.4 10.2 %collective-permute-start.6 = (f32[15,15,256]{2,1,0:T(8,128)S(1)}, f32[15,15,256]{2,1,0:T(8,128)S(1)}, u32[]{:S(2)}, u32[]{:S(2)}) collective-permute-start(f32[15,15,256]{2,1,0:T(8,128)S(1)} %slice_bitcast_fusion.1), channel_id=1, source_target_pairs={{1,0},{2,1},{3,2},{4,3},{5,4},{6,5},{7,6},{8,7},{9,8},{10,9},{11,1... | collective-permute-start | bytes 691208 | tf_op jit(solution)/shard_map/ppermute | solution.py:15
  183.7 7.7 %copy-start.1 = (f32[14,14,15,256]{3,2,1,0:T(8,128)S(1)}, f32[14,14,15,256]{3,2,1,0:T(8,128)}, u32[]{:S(2)}) copy-start(f32[14,14,15,256]{3,2,1,0:T(8,128)} %copy-done) | copy-start | bytes 9031684
  183.7 7.6 %collective-permute-start.7 = (f32[14,15,256]{2,1,0:T(8,128)S(1)}, f32[14,15,256]{2,1,0:T(8,128)S(1)}, u32[]{:S(2)}, u32[]{:S(2)}) collective-permute-start(f32[14,15,256]{2,1,0:T(8,128)S(1)} %slice_bitcast_fusion.5), channel_id=1, source_target_pairs={{16,0},{32,16},{48,32},{64,48},{80,64},{96,80},{112,96},{17,1},{33... | collective-permute-start | bytes 645128 | tf_op jit(solution)/shard_map/ppermute | solution.py:15
  191.4 1.8 copy-start.6
  193.2 3.7 collective-permute-start.8
  196.9 7.1 %collective-permute-start.9 = (bf16[15,15,256]{2,1,0:T(8,128)(2,1)S(1)}, bf16[15,15,256]{2,1,0:T(8,128)(2,1)S(1)}, u32[]{:S(2)}, u32[]{:S(2)}) collective-permute-start(bf16[15,15,256]{2,1,0:T(8,128)(2,1)S(1)} %fusion.25), channel_id=1, source_target_pairs={{0,1},{1,2},{2,3},{3,4},{4,5},{5,6},{6,7},{7,8},{8,9},{9,10},{10,1... | collective-permute-start | bytes 345608 | tf_op jit(solution)/shard_map/ppermute | solution.py:15
  225.1 2.8 copy-start.5
  262.5 11.3 %copy-start.12 = (f32[15,15,15,256]{3,2,1,0:T(8,128)S(1)}, f32[15,15,15,256]{3,2,1,0:T(8,128)}, u32[]{:S(2)}) copy-start(f32[15,15,15,256]{3,2,1,0:T(8,128)} %reshape.329) | copy-start | bytes 10368004
  263.7 10.2 %slice-start.2 = ((f32[15,15,15,256]{3,2,1,0:T(8,128)}), f32[15,14,15,256]{3,2,1,0:T(8,128)S(1)}, s32[]{:S(2)}) async-start(f32[15,15,15,256]{3,2,1,0:T(8,128)} %reshape.329), calls=%async_computation.3 | async-start | bytes 6881280 | tf_op jit(solution)/shard_map/slice | solution.py:43
  263.7 10.2 %collective-permute-start.10 = (f32[15,15,256]{2,1,0:T(8,128)S(1)}, f32[15,15,256]{2,1,0:T(8,128)S(1)}, u32[]{:S(2)}, u32[]{:S(2)}) collective-permute-start(f32[15,15,256]{2,1,0:T(8,128)S(1)} %slice_bitcast_fusion), channel_id=1, source_target_pairs={{1,0},{2,1},{3,2},{4,3},{5,4},{6,5},{7,6},{8,7},{9,8},{10,9},{11,1... | collective-permute-start | bytes 691208 | tf_op jit(solution)/shard_map/ppermute | solution.py:15
  265.2 16.3 %copy-start.9 = (bf16[14,14,13,256]{3,1,2,0:T(8,128)(2,1)S(1)}, bf16[14,14,13,256]{3,1,2,0:T(8,128)(2,1)}, u32[]{:S(2)}) copy-start(bf16[14,14,13,256]{3,1,2,0:T(8,128)(2,1)} %param.17) | copy-start | bytes 3913732
  273.9 7.7 %copy-start.2 = (f32[14,14,15,256]{3,2,1,0:T(8,128)S(1)}, f32[14,14,15,256]{3,2,1,0:T(8,128)}, u32[]{:S(2)}) copy-start(f32[14,14,15,256]{3,2,1,0:T(8,128)} %copy-done) | copy-start | bytes 9031684
  273.9 7.7 %copy-start.7 = (f32[14,14,15,256]{3,2,1,0:T(8,128)S(1)}, f32[14,14,15,256]{3,2,1,0:T(8,128)}, u32[]{:S(2)}) copy-start(f32[14,14,15,256]{3,2,1,0:T(8,128)} %copy-done.6) | copy-start | bytes 9031684
  273.9 7.6 %collective-permute-start.11 = (f32[14,15,256]{2,1,0:T(8,128)S(1)}, f32[14,15,256]{2,1,0:T(8,128)S(1)}, u32[]{:S(2)}, u32[]{:S(2)}) collective-permute-start(f32[14,15,256]{2,1,0:T(8,128)S(1)} %slice_bitcast_fusion.4), channel_id=1, source_target_pairs={{16,0},{32,16},{48,32},{64,48},{80,64},{96,80},{112,96},{17,1},{33... | collective-permute-start | bytes 645128 | tf_op jit(solution)/shard_map/ppermute | solution.py:15
  291.9 212.2 %copy-start.13 = (f32[2548,256]{1,0:T(8,128)S(1)}, f32[2548,256]{1,0:T(8,128)}, u32[]{:S(2)}) copy-start(f32[2548,256]{1,0:T(8,128)} %reshape.332) | copy-start | bytes 7827460
Sparse Core Ops, SparseCore 0:
  290.1 148.6 all-reduce.5
where the time goes:
time: 530 us; the launch traced here: 521 us
  waiting for transfers between devices  197 us (37%)
  other arithmetic  143 us (27%)
  local copies, waits for them, and re-layouts  111 us (21%)
  starting transfers between devices  33.3 us (6%)
  matrix products  21 us (4%)
  between operations  15.8 us (3%)
    psum x1, waiting for transfers between devices, shards(): gram_total = lax.psum(gram_local, ('dx', 'dy'))  147 us
    scatter-add x3, other arithmetic, apply_operator(): jnp.zeros((flat.shape[0], bands), jnp.float32).at[links]  72.1 us
    gather x3, local copies, waits for them, and re-layouts, apply_operator(): rows = jnp.take(flat, links, axis=0).reshape(count, nodes, bands)  51.1 us
    ppermute x12, waiting for transfers between devices, shifted(): return lax.ppermute(block, axis, route)  49.8 us
    another operation x6, other arithmetic, shards(): lower = jnp.linalg.cholesky(gram_total)  34.3 us
    ppermute x12, starting transfers between devices, shifted(): return lax.ppermute(block, axis, route)  33.3 us
    another operation x3, other arithmetic, shards(): lax.linalg.triangular_solve(lower, identity, left_side=True, lower=True)  20.5 us
    dot_general x3, local copies, waits for them, and re-layouts, apply_operator(): jnp.einsum('eij,ejb->eib', elem_mats.reshape(count, nodes, nodes), rows,...  16.2 us
  transfers between devices with their start and end apart: 13, of which 13 were waited for; matrix products, arithmetic and copies ran while one was open for 1% of the time, Pallas kernels for 0%

commit v1 on v0

v1 whole, which is shorter than its diff:
```python
import math

import jax
import jax.numpy as jnp
from jax import lax
from jax.experimental import pallas as pl
from jax.experimental.pallas import tpu as pltpu
from jax.sharding import PartitionSpec as P

MESH = pl.DeviceIdType.MESH
F32 = jnp.float32
BF16 = jnp.bfloat16
NB = 256
HI = lax.Precision.HIGHEST


def dot_nn(a, b, precision=None):
    return lax.dot_general(
        a, b, (((1,), (0,)), ((), ())), precision=precision, preferred_element_type=F32
    )


def dot_nt(a, b, precision=None):
    return lax.dot_general(
        a, b, (((1,), (1,)), ((), ())), precision=precision, preferred_element_type=F32
    )


def dot_tn(a, b, precision=None):
    return lax.dot_general(
        a, b, (((0,), (0,)), ((), ())), precision=precision, preferred_element_type=F32
    )


def filter_kernel(
    ndx, ndy,
    orb, mats, conn,
    yout, gout,
    abuf, ap, rmap, st, tt, ya, yb, acc,
    hx, hy, hc, sxl, sxh, syl, syh, rxl, rxh, ryl, ryh, rcs,
    gl, ra, sb, rb, gb, gf,
    msem, ysem, hss, hrs, ess, ers, as_, ar_, bs_, br_, cs_, cr_, ds_, dr_,
):
    dx = lax.axis_index("dx")
    dy = lax.axis_index("dy")
    xp, xm = lax.rem(dx + 1, ndx), lax.rem(dx + ndx - 1, ndx)
    yp, ym = lax.rem(dy + 1, ndy), lax.rem(dy + ndy - 1, ndy)

    barrier = pltpu.get_barrier_semaphore()
    partners = [(lax.rem(dx + d, ndx), dy) for d in range(1, ndx)]
    partners += [(dx, lax.rem(dy + d, ndy)) for d in range(1, ndy)]
    partners += [(xp, yp), (xp, ym), (xm, yp), (xm, ym)]
    for partner in partners:
        pl.semaphore_signal(barrier, inc=1, device_id=partner, device_id_type=MESH)

    loads = []
    for e in range(8):
        copy = pltpu.make_async_copy(mats.at[e // 4, e // 2 % 2, e % 2], abuf.at[e], msem.at[e])
        copy.start()
        loads.append(copy)

    m = lax.broadcasted_iota(jnp.int32, (512, 128), 0)
    a_of, b_of, s_of = m // 64, m // 8 % 8, m % 8
    plane = a_of * 225 + b_of * 15
    rmap[0] = jnp.where(s_of < 7, plane + s_of + 1, -1)
    rmap[1] = jnp.where(s_of < 5, plane + s_of + 2, jnp.where(s_of > 5, plane + s_of - 6, -1))

    ya[...] = jnp.zeros_like(ya)

    def fill(i, carry):
        ya[i + 1, 1:15, 0:13, :] = orb[i].astype(F32)
        return carry

    lax.fori_loop(0, 14, fill, 0)

    def fold(c):
        ex, ey = c // 2, c % 2
        links = conn[ex, ey]
        for ez in range(2):
            e = c * 2 + ez
            loads[e].wait()
            row = links[ez : ez + 1] - ((7 * ex * 15 + 7 * ey) * 15 + 7 * ez)
            for q in range(4):
                part = row[:, 128 * q : 128 * q + 128]
                st[:, 128 * q : 128 * q + 128] = jnp.where(rmap[ez] == part, 1.0, 0.0).astype(BF16)
            tt[...] = dot_nt(abuf[e], st[...]).astype(BF16)
            ap[e] = dot_nn(st[...], tt[...]).astype(BF16)

    def remote(src, dst, ssem, rsem, where):
        copy = pltpu.make_async_remote_copy(
            src_ref=src, dst_ref=dst, send_sem=ssem, recv_sem=rsem, device_id=where, device_id_type=MESH
        )
        copy.start()
        return copy

    fold(0)
    pl.semaphore_wait(barrier, len(partners))
    halo = [
        remote(orb.at[13], hx, hss.at[0], hrs.at[0], (xp, dy)),
        remote(orb.at[:, 13], hy, hss.at[1], hrs.at[1], (dx, yp)),
        remote(orb.at[13, 13], hc, hss.at[2], hrs.at[2], (xp, yp)),
    ]
    for c in range(1, 4):
        fold(c)
    for copy in halo:
        copy.wait()
    x_low, x_high, y_low, y_high = dx > 0, dx < ndx - 1, dy > 0, dy < ndy - 1
    ya[0, 1:15, 0:13, :] = jnp.where(x_low, hx[...].astype(F32), 0.0)
    ya[1:15, 0, 0:13, :] = jnp.where(y_low, hy[...].astype(F32), 0.0)
    ya[0, 0, 0:13, :] = jnp.where(jnp.logical_and(x_low, y_low), hc[...].astype(F32), 0.0)

    sub = lax.broadcasted_iota(jnp.int32, (8, 8, 8, NB), 2)
    first = sub < 6

    def apply(src):
        acc[...] = jnp.zeros_like(acc)
        for c in range(4):
            i0, j0 = 7 * (c // 2), 7 * (c % 2)
            t0 = src[i0 : i0 + 8, j0 : j0 + 8, 0:8, :]
            t1 = jnp.where(first, src[i0 : i0 + 8, j0 : j0 + 8, 8:16, :], t0)
            p0 = dot_nn(ap[2 * c], t0.reshape(512, NB).astype(BF16)).reshape(8, 8, 8, NB)
            p1 = dot_nn(ap[2 * c + 1], t1.reshape(512, NB).astype(BF16)).reshape(8, 8, 8, NB)
            acc[i0 : i0 + 8, j0 : j0 + 8, 0:8, :] += p0 + jnp.where(first, 0.0, p1)
            acc[i0 : i0 + 8, j0 : j0 + 8, 8:16, :] += jnp.where(first, p1, 0.0)

    def exchange(t):
        copies = []
        sxl[t] = acc[0].astype(BF16)
        copies.append(remote(sxl.at[t], rxh.at[t], ess.at[t, 0], ers.at[t, 0], (xm, dy)))
        syl[t] = acc[:, 0].astype(BF16)
        copies.append(remote(syl.at[t], ryh.at[t], ess.at[t, 1], ers.at[t, 1], (dx, ym)))
        copies.append(remote(sxl.at[t, 0], rcs.at[t, 0], ess.at[t, 2], ers.at[t, 2], (xm, ym)))
        if t < 2:
            sxh[t] = acc[14].astype(BF16)
            copies.append(remote(sxh.at[t], rxl.at[t], ess.at[t, 3], ers.at[t, 3], (xp, dy)))
            syh[t] = acc[:, 14].astype(BF16)
            copies.append(remote(syh.at[t], ryl.at[t], ess.at[t, 4], ers.at[t, 4], (dx, yp)))
            copies.append(remote(sxh.at[t, 14], rcs.at[t, 1], ess.at[t, 5], ers.at[t, 5], (xp, yp)))
            copies.append(remote(sxl.at[t, 14], rcs.at[t, 2], ess.at[t, 6], ers.at[t, 6], (xm, yp)))
            copies.append(remote(sxh.at[t, 0], rcs.at[t, 3], ess.at[t, 7], ers.at[t, 7], (xp, ym)))
        return copies

    def gated(flag, ref, coef):
        return jnp.where(flag, ref.astype(F32), 0.0) * coef

    def faces(t, y, coef):
        y[14] += gated(x_high, rxh[t], coef)
        y[:, 14] += gated(y_high, ryh[t], coef)
        y[14, 14] += gated(jnp.logical_and(x_high, y_high), rcs[t, 0], coef)
        if t < 2:
            y[0] += rxl[t].astype(F32) * coef
            y[:, 0] += ryl[t].astype(F32) * coef
            y[0, 0] += rcs[t, 1].astype(F32) * coef
            y[14, 0] += gated(x_high, rcs[t, 2], coef)
            y[0, 14] += gated(y_high, rcs[t, 3], coef)
            y[0] = jnp.where(x_low, y[0], 0.0)
            y[:, 0] = jnp.where(y_low, y[:, 0], 0.0)

    apply(ya)
    copies = exchange(0)
    yb[...] = 0.25 * acc[...] - 0.375 * ya[...]
    for copy in copies:
        copy.wait()
    faces(0, yb, 0.25)

    apply(yb)
    copies = exchange(1)
    ya[...] = 0.5 * acc[...] - 0.75 * yb[...] - ya[...]
    for copy in copies:
        copy.wait()
    faces(1, ya, 0.5)

    apply(ya)
    copies = exchange(2)
    yb[...] = 0.5 * acc[...] - 0.75 * ya[...] - yb[...]
    for copy in copies:
        copy.wait()
    faces(2, yb, 0.5)

    keep = pltpu.make_async_copy(yb.at[1:15, 1:15], yout, ysem)
    keep.start()

    for h in range(2):
        total = None
        for i in range(7):
            y = yb[1 + 2 * i : 3 + 2 * i, 1:15].reshape(448, NB)
            top = y.astype(BF16)
            low = (y - top.astype(F32)).astype(BF16)
            term = dot_tn(top, low if h else top)
            total = term if total is None else total + term
        if h == 0:
            gl[...] = total.reshape(8, 32, NB)
        else:
            gl[...] += (total + total.T).reshape(8, 32, NB)

    copies = []
    for d in range(1, ndx):
        peer = lax.rem(dx + d, ndx)
        copies.append(remote(gl.at[peer], ra.at[dx], as_.at[d], ar_.at[d], (peer, dy)))
    for copy in copies:
        copy.wait()
    chunk = gl[dx]
    for d in range(1, ndx):
        chunk += ra[lax.rem(dx + d, ndx)]
    for p in range(16):
        sb[p] = chunk[p // 2 * 4 : p // 2 * 4 + 4, p % 2 * 128 : p % 2 * 128 + 128]
    copies = []
    for d in range(1, ndy):
        peer = lax.rem(dy + d, ndy)
        copies.append(remote(sb.at[peer], rb.at[dy], bs_.at[d], br_.at[d], (dx, peer)))
    for copy in copies:
        copy.wait()
    piece = sb[dy]
    for d in range(1, ndy):
        piece += rb[lax.rem(dy + d, ndy)]
    gb[dy] = piece
    copies = []
    for d in range(1, ndy):
        peer = lax.rem(dy + d, ndy)
        copies.append(remote(gb.at[dy], gb.at[dy], cs_.at[d], cr_.at[d], (dx, peer)))
    for copy in copies:
        copy.wait()
    for p in range(16):
        gf[dx, p // 2 * 4 : p // 2 * 4 + 4, p % 2 * 128 : p % 2 * 128 + 128] = gb[p]
    copies = []
    for d in range(1, ndx):
        peer = lax.rem(dx + d, ndx)
        copies.append(remote(gf.at[dx], gf.at[dx], ds_.at[d], dr_.at[d], (peer, dy)))
    for copy in copies:
        copy.wait()
    gout[...] = gf[...].reshape(NB, NB)
    keep.wait()


def eliminate(tiles, n):
    count = n // 8
    rows = lax.broadcasted_iota(jnp.int32, (8, n), 0)
    lanes = lax.broadcasted_iota(jnp.int32, (8, n), 1)
    inverse = [jnp.where(lanes == rows + 8 * r, 1.0, 0.0) for r in range(count)]
    pivots = [jnp.ones((8, n), F32) for _ in range(count)]
    for k in range(n):
        r, j = k // 8, k % 8
        row = jnp.broadcast_to(tiles[r][j : j + 1, :], (8, n))
        pivot = jnp.broadcast_to(row[:, k : k + 1], (8, n))
        pivots[r] = jnp.where(rows == j, pivot, pivots[r])
        factor = 1.0 / pivot
        row = row * factor
        back = jnp.broadcast_to(inverse[r][j : j + 1, :], (8, n)) * factor
        for q in range(r, count):
            if q == r and j == 7:
                continue
            column = jnp.broadcast_to(tiles[q][:, k : k + 1], (8, n))
            if q == r:
                column = jnp.where(rows > j, column, 0.0)
            tiles[q] = tiles[q] - column * row
            inverse[q] = inverse[q] - column * back
    return jnp.concatenate([w * lax.rsqrt(p) for w, p in zip(inverse, pivots)], axis=0)


def basis_kernel(scale, y, g, out, ybuf, stage, whi, wlo, yin, osem):
    load = pltpu.make_async_copy(y, ybuf, yin)
    load.start()
    h = 128
    w1 = eliminate([g[8 * r : 8 * r + 8, 0:h] for r in range(16)], h)
    l21 = dot_nt(g[h:, 0:h], w1, HI)
    schur = g[h:, h:] - dot_nt(l21, l21, HI)
    mid = dot_nn(l21, w1, HI)
    w2 = eliminate([schur[8 * r : 8 * r + 8] for r in range(16)], h)
    w21 = -dot_nn(w2, mid, HI)

    def split(block, rows, cols):
        block = block * scale
        top = block.astype(BF16)
        whi[rows, cols] = top
        wlo[rows, cols] = (block - top.astype(F32)).astype(BF16)

    split(w1, slice(0, h), slice(0, h))
    split(jnp.zeros((h, h), F32), slice(0, h), slice(h, NB))
    split(w21, slice(h, NB), slice(0, h))
    split(w2, slice(h, NB), slice(h, NB))
    load.wait()
    copies = []
    for i in range(14):
        rows = ybuf[i].reshape(224, NB)
        top = rows.astype(BF16)
        low = (rows - top.astype(F32)).astype(BF16)
        q = dot_nt(top, whi[...]) + (dot_nt(top, wlo[...]) + dot_nt(low, whi[...]))
        stage[i] = q.reshape(14, 16, NB)[:, 0:13, :]
        copy = pltpu.make_async_copy(stage.at[i], out.at[i], osem.at[i])
        copy.start()
        copies.append(copy)
    for copy in copies:
        copy.wait()


def solution(mesh):
    ndx, ndy = mesh.shape["dx"], mesh.shape["dy"]
    vmem = pl.BlockSpec(memory_space=pltpu.VMEM)
    anywhere = pl.BlockSpec(memory_space=pl.ANY)
    scale = math.sqrt(14 * 14 * 13 * ndx * ndy)

    def shards(orbitals, elem_mats, conn):
        dma = pltpu.SemaphoreType.DMA
        y, g = pl.pallas_call(
            lambda *refs: filter_kernel(ndx, ndy, *refs),
            out_shape=(
                jax.ShapeDtypeStruct((14, 14, 16, NB), F32),
                jax.ShapeDtypeStruct((NB, NB), F32),
            ),
            in_specs=[vmem, anywhere, vmem],
            out_specs=(anywhere, vmem),
            scratch_shapes=[
                pltpu.VMEM((8, 512, 512), BF16),
                pltpu.VMEM((8, 512, 512), BF16),
                pltpu.VMEM((2, 512, 128), jnp.int32),
                pltpu.VMEM((512, 512), BF16),
                pltpu.VMEM((512, 512), BF16),
                pltpu.VMEM((15, 15, 16, NB), F32),
                pltpu.VMEM((15, 15, 16, NB), F32),
                pltpu.VMEM((15, 15, 16, NB), F32),
                pltpu.VMEM((14, 13, NB), BF16),
                pltpu.VMEM((14, 13, NB), BF16),
                pltpu.VMEM((13, NB), BF16),
                pltpu.VMEM((3, 15, 16, NB), BF16),
                pltpu.VMEM((2, 15, 16, NB), BF16),
                pltpu.VMEM((3, 15, 16, NB), BF16),
                pltpu.VMEM((2, 15, 16, NB), BF16),
                pltpu.VMEM((2, 15, 16, NB), BF16),
                pltpu.VMEM((3, 15, 16, NB), BF16),
                pltpu.VMEM((2, 15, 16, NB), BF16),
                pltpu.VMEM((3, 15, 16, NB), BF16),
                pltpu.VMEM((3, 4, 16, NB), BF16),
                pltpu.VMEM((8, 32, NB), F32),
                pltpu.VMEM((8, 32, NB), F32),
                pltpu.VMEM((16, 4, 128), F32),
                pltpu.VMEM((16, 4, 128), F32),
                pltpu.VMEM((16, 4, 128), F32),
                pltpu.VMEM((8, 32, NB), F32),
                dma((8,)),
                dma,
                dma((3,)),
                dma((3,)),
                dma((3, 8)),
                dma((3, 8)),
                dma((8,)),
                dma((8,)),
                dma((16,)),
                dma((16,)),
                dma((16,)),
                dma((16,)),
                dma((8,)),
                dma((8,)),
            ],
            compiler_params=pltpu.CompilerParams(collective_id=0, has_side_effects=True),
            name="filter",
        )(orbitals, elem_mats, conn)
        return pl.pallas_call(
            lambda *refs: basis_kernel(scale, *refs),
            out_shape=jax.ShapeDtypeStruct((14, 14, 13, NB), F32),
            in_specs=[anywhere, vmem],
            out_specs=anywhere,
            scratch_shapes=[
                pltpu.VMEM((14, 14, 16, NB), F32),
                pltpu.VMEM((14, 14, 13, NB), F32),
                pltpu.VMEM((NB, NB), BF16),
                pltpu.VMEM((NB, NB), BF16),
                dma,
                dma((14,)),
            ],
            name="basis",
        )(y, g)

    in_specs = (
        P("dx", "dy", None, None),
        P("dx", "dy", None, None, None),
        P("dx", "dy", None, None),
    )
    out_specs = P("dx", "dy", None, None)
    return jax.shard_map(shards, mesh=mesh, in_specs=in_specs, out_specs=out_specs, check_vma=False)
```

time: 530 us -> 111 us (0.21); the launches traced: 521 us -> 110 us
  waiting for transfers between devices: 197 us -> 0 us
  other arithmetic: 143 us -> 0 us
  local copies, waits for them, and re-layouts: 111 us -> 8.49 us
  Pallas kernels: 0 us -> 102 us
  starting transfers between devices: 33.3 us -> 0 us
  matrix products: 21 us -> 0 us
  between operations: 15.8 us -> 0.02 us
    psum x1 -> x0, waiting for transfers between devices: 147 us -> none  [shards(): gram_total = lax.psum(gram_local, ('dx', 'dy'))]
    pallas_call x0 -> x2, Pallas kernels: none -> 102 us  [the longest x1 61.3 us: shards(): pl.pallas_call(lambda *refs: filter_kernel(ndx, ndy, *refs), out_shape=(j...]
    scatter-add x9 -> x0, other arithmetic: 72.3 us -> none  [the longest x3 72.1 us: apply_operator(): jnp.zeros((flat.shape[0], bands), jnp.float32).at[links]]
    another operation x9 -> x0, other arithmetic: 54.8 us -> none  [the longest x6 34.3 us: shards(): lower = jnp.linalg.cholesky(gram_total)]
    gather x3 -> x0, local copies, waits for them, and re-layouts: 51.1 us -> none  [apply_operator(): rows = jnp.take(flat, links, axis=0).reshape(count, nodes, bands)]
    ppermute x12 -> x0, waiting for transfers between devices: 49.8 us -> none  [shifted(): return lax.ppermute(block, axis, route)]
    ppermute x12 -> x0, starting transfers between devices: 33.3 us -> none  [shifted(): return lax.ppermute(block, axis, route)]
    reshape x10 -> x0, local copies, waits for them, and re-layouts: 24.8 us -> none  [the longest x3 9.17 us: apply_operator(): summed = summed.reshape(width, width, depth, bands)]
  transfers between devices with their start and end apart: 13 -> 0, of which waited for: 13 -> 0; matrix products, arithmetic and copies ran while one was open for 1% -> 0% of each run, Pallas kernels for 0% -> 0%
where the time goes in v1:
time: 111 us; the launch traced here: 110 us
  Pallas kernels  102 us (92%)
  local copies, waits for them, and re-layouts  8.49 us (8%)
    pallas_call x1, Pallas kernels, shards(): pl.pallas_call(lambda *refs: filter_kernel(ndx, ndy, *refs), out_shape=(j...  61.3 us
    pallas_call x1, Pallas kernels, shards(): pl.pallas_call(lambda *refs: basis_kernel(scale, *refs), out_shape=jax.Sh...  40.5 us
    pallas_call x1, local copies, waits for them, and re-layouts, shards(): pl.pallas_call(lambda *refs: basis_kernel(scale, *refs), out_shape=jax.Sh...  5.39 us
    unnamed x1, local copies, waits for them, and re-layouts  3.1 us

profile of v1, /device:TPU:1, one launch (start us, length us, event | category | flops | bytes accessed | tf_op | source)
XLA Modules:
  0.0 110.3 jit_solution(11673268973214941225)
XLA Ops:
  0.0 3.1 %copy.4.refs_0_ = bf16[14,14,13,256]{3,2,1,0:T(8,128)(2,1)} copy(bf16[14,14,13,256]{3,1,2,0:T(8,128)(2,1)} %param.3) | data formatting | bytes 2609152 | tf_op args[0]
  3.1 61.3 %filter.1 = (f32[14,14,16,256]{3,2,1,0:T(8,128)}, f32[256,256]{1,0:T(8,128)}) custom-call(bf16[14,14,13,256]{3,2,1,0:T(8,128)(2,1)} %copy.4.refs_0_, bf16[2,2,2,512,512]{4,3,2,1,0:T(8,128)(2,1)} %refs_1_.1, s32[2,2,2,512]{3,2,1,0:T(2,128)} %refs_2_.1), custom_call_target="tpu_custom_call" | custom-call | tf_op jit(solution)/shard_map/filter/pallas_call | solution.py:304
  64.4 40.5 %basis.1 = f32[14,14,13,256]{3,2,1,0:T(8,128)} custom-call(f32[14,14,16,256]{3,2,1,0:T(8,128)} %get-tuple-element.7.refs_0_, f32[256,256]{1,0:T(8,128)} %get-tuple-element.8.refs_1_), custom_call_target="tpu_custom_call" | custom-call | tf_op jit(solution)/shard_map/basis/pallas_call | solution.py:357
  104.9 5.4 %copy.5 = f32[14,14,13,256]{3,1,2,0:T(8,128)} copy(f32[14,14,13,256]{3,2,1,0:T(8,128)} %basis.1) | data formatting | bytes 5218304 | tf_op jit(solution)/shard_map/basis/pallas_call | solution.py:357

commit v2 on v1

v2 whole, which is shorter than its diff:
```python
import math

import jax
import jax.numpy as jnp
from jax import lax
from jax.experimental import pallas as pl
from jax.experimental.pallas import tpu as pltpu
from jax.sharding import PartitionSpec as P

MESH = pl.DeviceIdType.MESH
F32 = jnp.float32
BF16 = jnp.bfloat16
NB = 256


def dot_nn(a, b, precision=None):
    return lax.dot_general(
        a, b, (((1,), (0,)), ((), ())), precision=precision, preferred_element_type=F32
    )


def dot_nt(a, b, precision=None):
    return lax.dot_general(
        a, b, (((1,), (1,)), ((), ())), precision=precision, preferred_element_type=F32
    )


def dot_tn(a, b, precision=None):
    return lax.dot_general(
        a, b, (((0,), (0,)), ((), ())), precision=precision, preferred_element_type=F32
    )


def filter_kernel(
    ndx, ndy,
    orb, mats, conn,
    yout, gout,
    abuf, ap, rmap, st, tt, ya2, yb2, acc2, both,
    hx, hy, hc, shy, shc, sxl, sxh, syl, syh, scs, rxl, rxh, ryl, ryh, rcs,
    gl, ra, sb, rb, gb, gf,
    msem, ysem, hss, hrs, ess, ers, as_, ar_, bs_, br_, cs_, cr_, ds_, dr_,
):
    dx = lax.axis_index("dx")
    dy = lax.axis_index("dy")
    xp, xm = lax.rem(dx + 1, ndx), lax.rem(dx + ndx - 1, ndx)
    yp, ym = lax.rem(dy + 1, ndy), lax.rem(dy + ndy - 1, ndy)
    ya, yb, acc = (ref.reshape(2, 15, 13, 16, 128) for ref in (ya2, yb2, acc2))

    barrier = pltpu.get_barrier_semaphore()
    partners = [(lax.rem(dx + d, ndx), dy) for d in range(1, ndx)]
    partners += [(dx, lax.rem(dy + d, ndy)) for d in range(1, ndy)]
    partners += [(xp, yp), (xp, ym), (xm, yp), (xm, ym)]
    for partner in partners:
        pl.semaphore_signal(barrier, inc=1, device_id=partner, device_id_type=MESH)

    loads = []
    for e in range(8):
        copy = pltpu.make_async_copy(mats.at[e // 4, e // 2 % 2, e % 2], abuf.at[e], msem.at[e])
        copy.start()
        loads.append(copy)

    grid = (8, 7, 8, 128)
    a_of, l_of, s_of = (lax.broadcasted_iota(jnp.int32, grid, d) for d in range(3))
    for ey in range(2):
        b_of = jnp.where(s_of < 7 - ey, s_of + 1 + ey, s_of - 7 + ey)
        rmap[ey] = (a_of * 225 + b_of * 15 + l_of).reshape(448, 128)

    ya2[...] = jnp.zeros_like(ya2)

    def fill(i, carry):
        plane = orb[i].astype(F32)
        for h in range(2):
            ya[h, i + 1, :, 0:14, :] = plane[:, :, 128 * h : 128 * h + 128]
        return carry

    lax.fori_loop(0, 14, fill, 0)

    def line(i, slot, count):
        return pl.ds(i * 208 + slot, 13 * count, stride=16)

    for h in range(2):
        shy[h] = ya2[h, line(1, 13, 14), :].astype(BF16)
        shc[h] = ya2[h, line(14, 13, 1), :].astype(BF16)

    def fold(c):
        ex, ey = c // 2, c % 2
        links = conn[ex, ey]
        for ez in range(2):
            e = c * 2 + ez
            loads[e].wait()
            row = links[ez : ez + 1] - ((7 * ex * 15 + 7 * ey) * 15 + 7 * ez + 1 - ez)
            for q in range(4):
                part = row[:, 128 * q : 128 * q + 128]
                st[:, 128 * q : 128 * q + 128] = jnp.where(rmap[ey] == part, 1.0, 0.0).astype(BF16)
            tt[...] = dot_nt(abuf[e], st[...]).astype(BF16)
            ap[e] = dot_nn(st[...], tt[...]).astype(BF16)

    def remote(src, dst, ssem, rsem, where):
        copy = pltpu.make_async_remote_copy(
            src_ref=src, dst_ref=dst, send_sem=ssem, recv_sem=rsem, device_id=where, device_id_type=MESH
        )
        copy.start()
        return copy

    fold(0)
    pl.semaphore_wait(barrier, len(partners))
    halo = [
        remote(orb.at[13], hx, hss.at[0], hrs.at[0], (xp, dy)),
        remote(shy, hy, hss.at[1], hrs.at[1], (dx, yp)),
        remote(shc, hc, hss.at[2], hrs.at[2], (xp, yp)),
    ]
    for c in range(1, 4):
        fold(c)
    for copy in halo:
        copy.wait()
    x_low, x_high, y_low, y_high = dx > 0, dx < ndx - 1, dy > 0, dy < ndy - 1
    plane = jnp.where(x_low, hx[...].astype(F32), 0.0)
    for h in range(2):
        ya[h, 0, :, 0:14, :] = plane[:, :, 128 * h : 128 * h + 128]
        ya2[h, line(1, 15, 14), :] = jnp.where(y_low, hy[h].astype(F32), 0.0)
        ya2[h, line(0, 15, 1), :] = jnp.where(
            jnp.logical_and(x_low, y_low), hc[h].astype(F32), 0.0
        )

    sub = lax.broadcasted_iota(jnp.int32, (8, 7, 8, 128), 2)

    def apply(src):
        acc2[...] = jnp.zeros_like(acc2)
        for ex in range(2):
            for ez in range(2):
                box = (slice(7 * ex, 7 * ex + 8), slice(6 * ez, 6 * ez + 7))
                t0, t1 = [], []
                for h in range(2):
                    n0 = src[(h, *box, slice(0, 8))]
                    n1 = src[(h, *box, slice(8, 16))]
                    t0.append(jnp.where(sub < 7, n0, n1).reshape(448, 128).astype(BF16))
                    t1.append(jnp.where(sub < 6, n1, n0).reshape(448, 128).astype(BF16))
                q0 = dot_nn(ap[4 * ex + ez], jnp.concatenate(t0, axis=1))
                q1 = dot_nn(ap[4 * ex + 2 + ez], jnp.concatenate(t1, axis=1))
                for h in range(2):
                    p0, p1 = (
                        q[:, 128 * h : 128 * h + 128].reshape(8, 7, 8, 128) for q in (q0, q1)
                    )
                    acc[(h, *box, slice(0, 8))] += jnp.where(sub < 7, p0, 0.0) + jnp.where(
                        sub < 6, 0.0, p1
                    )
                    acc[(h, *box, slice(8, 16))] += jnp.where(sub < 6, p1, 0.0) + jnp.where(
                        sub < 7, 0.0, p0
                    )

    def exchange(t):
        copies = []
        for h in range(2):
            syl[t, h] = acc2[h, line(0, 15, 15), :].astype(BF16)
        copies.append(remote(syl.at[t], ryh.at[t], ess.at[t, 1], ers.at[t, 1], (dx, ym)))
        if t < 2:
            for h in range(2):
                syh[t, h] = acc2[h, line(0, 13, 15), :].astype(BF16)
            copies.append(remote(syh.at[t], ryl.at[t], ess.at[t, 4], ers.at[t, 4], (dx, yp)))
        sxl[t] = acc[:, 0].astype(BF16)
        copies.append(remote(sxl.at[t], rxh.at[t], ess.at[t, 0], ers.at[t, 0], (xm, dy)))
        if t < 2:
            sxh[t] = acc[:, 14].astype(BF16)
            copies.append(remote(sxh.at[t], rxl.at[t], ess.at[t, 3], ers.at[t, 3], (xp, dy)))
        corners = [(0, 15, (xm, ym)), (14, 13, (xp, yp)), (0, 13, (xm, yp)), (14, 15, (xp, ym))]
        for n, (i, slot, where) in enumerate(corners[: 4 if t < 2 else 1]):
            for h in range(2):
                scs[t, n, h] = acc2[h, line(i, slot, 1), :].astype(BF16)
            copies.append(remote(scs.at[t, n], rcs.at[t, n], ess.at[t, 5 + n], ers.at[t, 5 + n], where))
        return copies

    def gated(flag, value, coef):
        return jnp.where(flag, value.astype(F32), 0.0) * coef

    def faces(t, y, y2, coef):
        def bump(i, slot, count, value):
            for h in range(2):
                y2[h, line(i, slot, count), :] += value[h]

        y[:, 14] += gated(x_high, rxh[t], coef)
        bump(0, 13, 15, gated(y_high, ryh[t], coef))
        bump(14, 13, 1, gated(jnp.logical_and(x_high, y_high), rcs[t, 0], coef))
        if t < 2:
            y[:, 0] += rxl[t].astype(F32) * coef
            bump(0, 15, 15, ryl[t].astype(F32) * coef)
            bump(0, 15, 1, rcs[t, 1].astype(F32) * coef)
            bump(14, 15, 1, gated(x_high, rcs[t, 2], coef))
            bump(0, 13, 1, gated(y_high, rcs[t, 3], coef))
            y[:, 0] = jnp.where(x_low, y[:, 0], 0.0)
            for h in range(2):
                edge = y2[h, line(0, 15, 15), :]
                y2[h, line(0, 15, 15), :] = jnp.where(y_low, edge, 0.0)

    apply(ya)
    copies = exchange(0)
    yb2[...] = 0.25 * acc2[...] - 0.375 * ya2[...]
    for copy in copies:
        copy.wait()
    faces(0, yb, yb2, 0.25)

    apply(yb)
    copies = exchange(1)
    ya2[...] = 0.5 * acc2[...] - 0.75 * yb2[...] - ya2[...]
    for copy in copies:
        copy.wait()
    faces(1, ya, ya2, 0.5)

    apply(ya)
    copies = exchange(2)
    yb2[...] = 0.5 * acc2[...] - 0.75 * ya2[...] - yb2[...]
    for copy in copies:
        copy.wait()
    faces(2, yb, yb2, 0.5)
    for h in range(2):
        yb2[h, line(0, 15, 15), :] = jnp.zeros((195, 128), F32)

    for h in range(2):
        y = yb2[h, 208:3120, :]
        top = y.astype(BF16)
        both[:, 128 * h : 128 * h + 128] = top
        both[:, NB + 128 * h : NB + 128 * h + 128] = (y - top.astype(F32)).astype(BF16)
    keep = pltpu.make_async_copy(both, yout, ysem)
    keep.start()
    total = dot_tn(both[:, 0:NB], both[...])
    cross = total[:, NB:]
    gl[...] = (total[:, 0:NB] + (cross + cross.T)).reshape(8, 32, NB)

    copies = []
    for d in range(1, ndx):
        peer = lax.rem(dx + d, ndx)
        copies.append(remote(gl.at[peer], ra.at[dx], as_.at[d], ar_.at[d], (peer, dy)))
    for copy in copies:
        copy.wait()
    chunk = gl[dx]
    for d in range(1, ndx):
        chunk += ra[lax.rem(dx + d, ndx)]
    for p in range(16):
        sb[p] = chunk[p // 2 * 4 : p // 2 * 4 + 4, p % 2 * 128 : p % 2 * 128 + 128]
    copies = []
    for d in range(1, ndy):
        peer = lax.rem(dy + d, ndy)
        copies.append(remote(sb.at[peer], rb.at[dy], bs_.at[d], br_.at[d], (dx, peer)))
    for copy in copies:
        copy.wait()
    piece = sb[dy]
    for d in range(1, ndy):
        piece += rb[lax.rem(dy + d, ndy)]
    gb[dy] = piece
    copies = []
    for d in range(1, ndy):
        peer = lax.rem(dy + d, ndy)
        copies.append(remote(gb.at[dy], gb.at[dy], cs_.at[d], cr_.at[d], (dx, peer)))
    for copy in copies:
        copy.wait()
    for p in range(16):
        gf[dx, p // 2 * 4 : p // 2 * 4 + 4, p % 2 * 128 : p % 2 * 128 + 128] = gb[p]
    copies = []
    for d in range(1, ndx):
        peer = lax.rem(dx + d, ndx)
        copies.append(remote(gf.at[dx], gf.at[dx], ds_.at[d], dr_.at[d], (peer, dy)))
    for copy in copies:
        copy.wait()
    gout[...] = gf[...].reshape(NB, NB)
    keep.wait()


def split3(x):
    a = x.astype(BF16)
    rest = x - a.astype(F32)
    b = rest.astype(BF16)
    return a, b, (rest - b.astype(F32)).astype(BF16)


def factor_inverse(g, work):
    rows = lax.broadcasted_iota(jnp.int32, (8, 128), 0)
    lanes = lax.broadcasted_iota(jnp.int32, (8, 128), 1)
    scales = []
    for o in range(8):
        base = 32 * o
        source = g if o == 0 else work
        tiles = [
            [source[base + 8 * t : base + 8 * t + 8, 128 * h : 128 * h + 128] for h in range(2)]
            for t in range(4)
        ]
        factors = []
        half = base // 128
        for s in range(4):
            first = base + 8 * s - 128 * half
            inside = jnp.logical_and(lanes >= first, lanes < first + 8)
            columns = []
            for q in range(s, 4):
                tile = tiles[q][half]
                columns.append(
                    [jnp.broadcast_to(tile[:, first + j : first + j + 1], (8, 128)) for j in range(8)]
                )
                fresh = jnp.where(lanes == rows + first, 1.0, 0.0) if q == s else 0.0
                tiles[q][half] = jnp.where(inside, fresh, tile)
            scale = jnp.ones((8, 128), F32)
            factor = jnp.ones((8, 128), F32)
            for k in range(8):
                lead = [jnp.broadcast_to(columns[0][j][k : k + 1, :], (8, 128)) for j in range(k, 8)]
                inv = 1.0 / lead[0]
                scale = jnp.where(rows == k, lead[0], scale)
                factor = jnp.where(rows == k, inv, factor)
                pivot = [jnp.broadcast_to(tiles[s][h][k : k + 1, :], (8, 128)) * inv for h in range(2)]
                lead = [v * inv for v in lead]
                for q in range(s, 4):
                    if q == s and k == 7:
                        continue
                    column = columns[q - s][k]
                    if q == s:
                        column = jnp.where(rows > k, column, 0.0)
                    for j in range(k + 1, 8):
                        columns[q - s][j] = columns[q - s][j] - column * lead[j - k]
                    for h in range(2):
                        tiles[q][h] = tiles[q][h] - column * pivot[h]
            scales.append(lax.rsqrt(scale))
            factors.append(factor)
        for t in range(4):
            for h in range(2):
                work[base + 8 * t : base + 8 * t + 8, 128 * h : 128 * h + 128] = tiles[t][h]
        if o < 7:
            u = jnp.concatenate([jnp.concatenate(tiles[t], axis=1) for t in range(4)], axis=0)
            f = jnp.concatenate([jnp.concatenate([v, v], axis=1) for v in factors], axis=0)
            r = lax.broadcasted_iota(jnp.int32, (32, NB), 0) + base
            c = lax.broadcasted_iota(jnp.int32, (32, NB), 1)
            v = jnp.where(jnp.logical_and(c > r, c < base + 32), 0.0, u * f)
            start = 128 * ((base + 32) // 128)
            u1, u2, u3 = split3(u[:, start:])
            v1, v2, v3 = split3(v)
            left = jnp.concatenate([u1, u1, u1, u2, u2, u3], axis=0)
            right = jnp.concatenate([v1, v2, v3, v1, v2, v1], axis=0)
            change = lax.dot_general(
                left, right, (((0,), (0,)), ((), ())), preferred_element_type=F32
            )
            rest = slice(base + 32, NB)
            old = (g if o == 0 else work)[rest, :]
            cc = lax.broadcasted_iota(jnp.int32, old.shape, 1)
            old = jnp.where(jnp.logical_and(cc >= base, cc < base + 32), 0.0, old)
            work[rest, :] = old - change[base + 32 - start :, :]
    for t in range(32):
        for h in range(2):
            tile = work[8 * t : 8 * t + 8, 128 * h : 128 * h + 128] * scales[t]
            work[8 * t : 8 * t + 8, 128 * h : 128 * h + 128] = jnp.where(
                lanes + 128 * h <= rows + 8 * t, tile, 0.0
            )


def basis_kernel(scale, y, g, out, ybuf, stage, work, whh, wlo, yin, osem):
    load = pltpu.make_async_copy(y, ybuf, yin)
    load.start()
    factor_inverse(g, work)
    w = work[...] * scale
    top = w.astype(BF16)
    whh[:, 0:NB] = top
    whh[:, NB:] = top
    wlo[...] = (w - top.astype(F32)).astype(BF16)
    load.wait()
    copies = []
    for i in range(14):
        rows = slice(208 * i, 208 * i + 208)
        q = dot_nt(ybuf[rows, :], whh[...]) + dot_nt(ybuf[rows, 0:NB], wlo[...])
        stage[i] = q.reshape(13, 16, NB)[:, 0:14, :]
        copy = pltpu.make_async_copy(stage.at[i], out.at[i], osem.at[i])
        copy.start()
        copies.append(copy)
    for copy in copies:
        copy.wait()


def solution(mesh):
    ndx, ndy = mesh.shape["dx"], mesh.shape["dy"]
    vmem = pl.BlockSpec(memory_space=pltpu.VMEM)
    anywhere = pl.BlockSpec(memory_space=pl.ANY)
    scale = math.sqrt(14 * 14 * 13 * ndx * ndy)

    def shards(orbitals, elem_mats, conn):
        dma = pltpu.SemaphoreType.DMA
        y, g = pl.pallas_call(
            lambda *refs: filter_kernel(ndx, ndy, *refs),
            out_shape=(
                jax.ShapeDtypeStruct((2912, 2 * NB), BF16),
                jax.ShapeDtypeStruct((NB, NB), F32),
            ),
            in_specs=[vmem, anywhere, vmem],
            out_specs=(anywhere, vmem),
            scratch_shapes=[
                pltpu.VMEM((8, 512, 512), BF16),
                pltpu.VMEM((8, 448, 448), BF16),
                pltpu.VMEM((2, 448, 128), jnp.int32),
                pltpu.VMEM((448, 512), BF16),
                pltpu.VMEM((512, 448), BF16),
                pltpu.VMEM((2, 3120, 128), F32),
                pltpu.VMEM((2, 3120, 128), F32),
                pltpu.VMEM((2, 3120, 128), F32),
                pltpu.VMEM((2912, 2 * NB), BF16),
                pltpu.VMEM((13, 14, NB), BF16),
                pltpu.VMEM((2, 182, 128), BF16),
                pltpu.VMEM((2, 13, 128), BF16),
                pltpu.VMEM((2, 182, 128), BF16),
                pltpu.VMEM((2, 13, 128), BF16),
                pltpu.VMEM((3, 2, 13, 16, 128), BF16),
                pltpu.VMEM((2, 2, 13, 16, 128), BF16),
                pltpu.VMEM((3, 2, 195, 128), BF16),
                pltpu.VMEM((2, 2, 195, 128), BF16),
                pltpu.VMEM((3, 4, 2, 13, 128), BF16),
                pltpu.VMEM((2, 2, 13, 16, 128), BF16),
                pltpu.VMEM((3, 2, 13, 16, 128), BF16),
                pltpu.VMEM((2, 2, 195, 128), BF16),
                pltpu.VMEM((3, 2, 195, 128), BF16),
                pltpu.VMEM((3, 4, 2, 13, 128), BF16),
                pltpu.VMEM((8, 32, NB), F32),
                pltpu.VMEM((8, 32, NB), F32),
                pltpu.VMEM((16, 4, 128), F32),
                pltpu.VMEM((16, 4, 128), F32),
                pltpu.VMEM((16, 4, 128), F32),
                pltpu.VMEM((8, 32, NB), F32),
                dma((8,)),
                dma,
                dma((3,)),
                dma((3,)),
                dma((3, 9)),
                dma((3, 9)),
                dma((8,)),
                dma((8,)),
                dma((16,)),
                dma((16,)),
                dma((16,)),
                dma((16,)),
                dma((8,)),
                dma((8,)),
            ],
            compiler_params=pltpu.CompilerParams(collective_id=0, has_side_effects=True),
            name="filter",
        )(jnp.swapaxes(orbitals, 1, 2), elem_mats, conn)
        filtered = pl.pallas_call(
            lambda *refs: basis_kernel(scale, *refs),
            out_shape=jax.ShapeDtypeStruct((14, 13, 14, NB), F32),
            in_specs=[anywhere, vmem],
            out_specs=anywhere,
            scratch_shapes=[
                pltpu.VMEM((2912, 2 * NB), BF16),
                pltpu.VMEM((14, 13, 14, NB), F32),
                pltpu.VMEM((NB, NB), F32),
                pltpu.VMEM((NB, 2 * NB), BF16),
                pltpu.VMEM((NB, NB), BF16),
                dma,
                dma((14,)),
            ],
            name="basis",
        )(y, g)
        return jnp.swapaxes(filtered, 1, 2)

    in_specs = (
        P("dx", "dy", None, None),
        P("dx", "dy", None, None, None),
        P("dx", "dy", None, None),
    )
    out_specs = P("dx", "dy", None, None)
    return jax.shard_map(shards, mesh=mesh, in_specs=in_specs, out_specs=out_specs, check_vma=False)
```

time: 111 us -> 73.8 us (0.66)
  Pallas kernels: 102 us -> 73.4 us
  local copies, waits for them, and re-layouts: 8.49 us -> 0 us
    pallas_call x1, Pallas kernels: 40.5 us -> 12.5 us  [shards(): pl.pallas_call(lambda *refs: basis_kernel(scale, *refs), out_shape=jax.Sh...]
    pallas_call x1 -> x0, local copies, waits for them, and re-layouts: 5.39 us -> none  [shards(): pl.pallas_call(lambda *refs: basis_kernel(scale, *refs), out_shape=jax.Sh...]
    unnamed x1 -> x0, local copies, waits for them, and re-layouts: 3.1 us -> none
where the time goes in v2:
time: 73.8 us; the launch traced here: 73.6 us
  Pallas kernels  73.4 us (99%)
    pallas_call x1, Pallas kernels, shards(): pl.pallas_call(lambda *refs: filter_kernel(ndx, ndy, *refs), out_shape=(j...  60.9 us
    pallas_call x1, Pallas kernels, shards(): pl.pallas_call(lambda *refs: basis_kernel(scale, *refs), out_shape=jax.Sh...  12.5 us

profile of v2, /device:TPU:1, one launch (start us, length us, event | category | flops | bytes accessed | tf_op | source)
XLA Modules:
  0.0 73.6 jit_solution(5293920969862511082)
XLA Ops:
  0.0 60.9 %filter.1 = (bf16[2912,512]{1,0:T(8,128)(2,1)}, f32[256,256]{1,0:T(8,128)}) custom-call(bf16[14,13,14,256]{3,2,1,0:T(8,128)(2,1)} %bitcast.2, bf16[2,2,2,512,512]{4,3,2,1,0:T(8,128)(2,1)} %refs_1_.1, s32[2,2,2,512]{3,2,1,0:T(2,128)} %refs_2_.1), custom_call_target="tpu_custom_call" | custom-call | tf_op jit(solution)/shard_map/filter/pallas_call | solution.py:379
  60.9 12.5 %basis.1 = f32[14,13,14,256]{3,2,1,0:T(8,128)} custom-call(bf16[2912,512]{1,0:T(8,128)(2,1)} %get-tuple-element.7.refs_0_, f32[256,256]{1,0:T(8,128)} %get-tuple-element.8.refs_1_), custom_call_target="tpu_custom_call" | custom-call | tf_op jit(solution)/shard_map/basis/pallas_call | solution.py:436

commit v3 on v2

--- a/solution.py
+++ b/solution.py
@@ -104,126 +104,148 @@
 
     fold(0)
     pl.semaphore_wait(barrier, len(partners))
-    halo = [
-        remote(orb.at[13], hx, hss.at[0], hrs.at[0], (xp, dy)),
-        remote(shy, hy, hss.at[1], hrs.at[1], (dx, yp)),
-        remote(shc, hc, hss.at[2], hrs.at[2], (xp, yp)),
-    ]
+    halo = []
+    for h in range(2):
+        half = orb.at[13, :, :, 128 * h : 128 * h + 128]
+        halo.append(
+            [
+                remote(shy.at[h], hy.at[h], hss.at[h, 1], hrs.at[h, 1], (dx, yp)),
+                remote(half, hx.at[h], hss.at[h, 0], hrs.at[h, 0], (xp, dy)),
+                remote(shc.at[h], hc.at[h], hss.at[h, 2], hrs.at[h, 2], (xp, yp)),
+            ]
+        )
     for c in range(1, 4):
         fold(c)
-    for copy in halo:
-        copy.wait()
     x_low, x_high, y_low, y_high = dx > 0, dx < ndx - 1, dy > 0, dy < ndy - 1
-    plane = jnp.where(x_low, hx[...].astype(F32), 0.0)
-    for h in range(2):
-        ya[h, 0, :, 0:14, :] = plane[:, :, 128 * h : 128 * h + 128]
+
+    sub = lax.broadcasted_iota(jnp.int32, (8, 7, 8, 128), 2)
+
+    def apply(src, h):
+        for ex in range(2):
+            for ez in range(2):
+                i0, l0 = 7 * ex, 6 * ez
+                rows, layers = slice(i0, i0 + 8), slice(l0, l0 + 7)
+                n0 = src[h, rows, layers, 0:8]
+                n1 = src[h, rows, layers, 8:16]
+                t0 = jnp.where(sub < 7, n0, n1).reshape(448, 128).astype(BF16)
+                t1 = jnp.where(sub < 6, n1, n0).reshape(448, 128).astype(BF16)
+                p0 = dot_nn(ap[4 * ex + ez], t0).reshape(8, 7, 8, 128)
+                p1 = dot_nn(ap[4 * ex + 2 + ez], t1).reshape(8, 7, 8, 128)
+                m0 = jnp.where(sub < 7, p0, 0.0) + jnp.where(sub < 6, 0.0, p1)
+                m1 = jnp.where(sub < 6, p1, 0.0) + jnp.where(sub < 7, 0.0, p0)
+                for part, tile in ((m0, slice(0, 8)), (m1, slice(8, 16))):
+                    if ex:
+                        first = part[:1, ez:] + acc[h, 7:8, l0 + ez : l0 + 7, tile]
+                        rest = jnp.concatenate([first, part[1:, ez:]], axis=0)
+                    else:
+                        rest = part[:, ez:]
+                    if ez:
+                        joint = part[:, :1] + acc[h, rows, l0 : l0 + 1, tile]
+                        rest = jnp.concatenate([joint, rest], axis=1)
+                    acc[h, rows, layers, tile] = rest
+
+    def exchange(t, h):
+        copies = []
+
+        def send(n, src, dst, where):
+            copies.append(remote(src, dst, ess.at[t, h, n], ers.at[t, h, n], where))
+
+        syl[t, h] = acc2[h, line(0, 15, 15), :].astype(BF16)
+        send(0, syl.at[t, h], ryh.at[t, h], (dx, ym))
+        if t < 2:
+            syh[t, h] = acc2[h, line(0, 13, 15), :].astype(BF16)
+            send(1, syh.at[t, h], ryl.at[t, h], (dx, yp))
+        sxl[t, h] = acc[h, 0].astype(BF16)
+        send(2, sxl.at[t, h], rxh.at[t, h], (xm, dy))
+        if t < 2:
+            sxh[t, h] = acc[h, 14].astype(BF16)
+            send(3, sxh.at[t, h], rxl.at[t, h], (xp, dy))
+        corners = [(0, 15, (xm, ym)), (14, 13, (xp, yp)), (0, 13, (xm, yp)), (14, 15, (xp, ym))]
+        for n, (i, slot, where) in enumerate(corners[: 4 if t < 2 else 1]):
+            scs[t, n, h] = acc2[h, line(i, slot, 1), :].astype(BF16)
+            send(4 + n, scs.at[t, n, h], rcs.at[t, n, h], where)
+        return copies
+
+    def gated(flag, value, coef):
+        return jnp.where(flag, value.astype(F32), 0.0) * coef
+
+    def faces(t, h, y, y2, coef):
+        def bump(i, slot, count, value):
+            y2[h, line(i, slot, count), :] += value
+
+        y[h, 14] += gated(x_high, rxh[t, h], coef)
+        bump(0, 13, 15, gated(y_high, ryh[t, h], coef))
+        bump(14, 13, 1, gated(jnp.logical_and(x_high, y_high), rcs[t, 0, h], coef))
+        if t < 2:
+            y[h, 0] += rxl[t, h].astype(F32) * coef
+            bump(0, 15, 15, ryl[t, h].astype(F32) * coef)
+            bump(0, 15, 1, rcs[t, 1, h].astype(F32) * coef)
+            bump(14, 15, 1, gated(x_high, rcs[t, 2, h], coef))
+            bump(0, 13, 1, gated(y_high, rcs[t, 3, h], coef))
+            y[h, 0] = jnp.where(x_low, y[h, 0], 0.0)
+            edge = y2[h, line(0, 15, 15), :]
+            y2[h, line(0, 15, 15), :] = jnp.where(y_low, edge, 0.0)
+
+    def wait(copies):
+        for copy in copies:
+            copy.wait()
+
+    stages = []
+    for h in range(2):
+        wait(halo[h])
+        ya[h, 0, :, 0:14, :] = jnp.where(x_low, hx[h].astype(F32), 0.0)
         ya2[h, line(1, 15, 14), :] = jnp.where(y_low, hy[h].astype(F32), 0.0)
         ya2[h, line(0, 15, 1), :] = jnp.where(
             jnp.logical_and(x_low, y_low), hc[h].astype(F32), 0.0
         )
-
-    sub = lax.broadcasted_iota(jnp.int32, (8, 7, 8, 128), 2)
-
-    def apply(src):
-        acc2[...] = jnp.zeros_like(acc2)
-        for ex in range(2):
-            for ez in range(2):
-                box = (slice(7 * ex, 7 * ex + 8), slice(6 * ez, 6 * ez + 7))
-                t0, t1 = [], []
-                for h in range(2):
-                    n0 = src[(h, *box, slice(0, 8))]
-                    n1 = src[(h, *box, slice(8, 16))]
-                    t0.append(jnp.where(sub < 7, n0, n1).reshape(448, 128).astype(BF16))
-                    t1.append(jnp.where(sub < 6, n1, n0).reshape(448, 128).astype(BF16))
-                q0 = dot_nn(ap[4 * ex + ez], jnp.concatenate(t0, axis=1))
-                q1 = dot_nn(ap[4 * ex + 2 + ez], jnp.concatenate(t1, axis=1))
-                for h in range(2):
-                    p0, p1 = (
-                        q[:, 128 * h : 128 * h + 128].reshape(8, 7, 8, 128) for q in (q0, q1)
-                    )
-                    acc[(h, *box, slice(0, 8))] += jnp.where(sub < 7, p0, 0.0) + jnp.where(
-                        sub < 6, 0.0, p1
-                    )
-                    acc[(h, *box, slice(8, 16))] += jnp.where(sub < 6, p1, 0.0) + jnp.where(
-                        sub < 7, 0.0, p0
-                    )
-
-    def exchange(t):
-        copies = []
-        for h in range(2):
-            syl[t, h] = acc2[h, line(0, 15, 15), :].astype(BF16)
-        copies.append(remote(syl.at[t], ryh.at[t], ess.at[t, 1], ers.at[t, 1], (dx, ym)))
-        if t < 2:
-            for h in range(2):
-                syh[t, h] = acc2[h, line(0, 13, 15), :].astype(BF16)
-            copies.append(remote(syh.at[t], ryl.at[t], ess.at[t, 4], ers.at[t, 4], (dx, yp)))
-        sxl[t] = acc[:, 0].astype(BF16)
-        copies.append(remote(sxl.at[t], rxh.at[t], ess.at[t, 0], ers.at[t, 0], (xm, dy)))
-        if t < 2:
-            sxh[t] = acc[:, 14].astype(BF16)
-            copies.append(remote(sxh.at[t], rxl.at[t], ess.at[t, 3], ers.at[t, 3], (xp, dy)))
-        corners = [(0, 15, (xm, ym)), (14, 13, (xp, yp)), (0, 13, (xm, yp)), (14, 15, (xp, ym))]
-        for n, (i, slot, where) in enumerate(corners[: 4 if t < 2 else 1]):
-            for h in range(2):
-                scs[t, n, h] = acc2[h, line(i, slot, 1), :].astype(BF16)
-            copies.append(remote(scs.at[t, n], rcs.at[t, n], ess.at[t, 5 + n], ers.at[t, 5 + n], where))
-        return copies
-
-    def gated(flag, value, coef):
-        return jnp.where(flag, value.astype(F32), 0.0) * coef
-
-    def faces(t, y, y2, coef):
-        def bump(i, slot, count, value):
-            for h in range(2):
-                y2[h, line(i, slot, count), :] += value[h]
-
-        y[:, 14] += gated(x_high, rxh[t], coef)
-        bump(0, 13, 15, gated(y_high, ryh[t], coef))
-        bump(14, 13, 1, gated(jnp.logical_and(x_high, y_high), rcs[t, 0], coef))
-        if t < 2:
-            y[:, 0] += rxl[t].astype(F32) * coef
-            bump(0, 15, 15, ryl[t].astype(F32) * coef)
-            bump(0, 15, 1, rcs[t, 1].astype(F32) * coef)
-            bump(14, 15, 1, gated(x_high, rcs[t, 2], coef))
-            bump(0, 13, 1, gated(y_high, rcs[t, 3], coef))
-            y[:, 0] = jnp.where(x_low, y[:, 0], 0.0)
-            for h in range(2):
-                edge = y2[h, line(0, 15, 15), :]
-                y2[h, line(0, 15, 15), :] = jnp.where(y_low, edge, 0.0)
-
-    apply(ya)
-    copies = exchange(0)
-    yb2[...] = 0.25 * acc2[...] - 0.375 * ya2[...]
-    for copy in copies:
-        copy.wait()
-    faces(0, yb, yb2, 0.25)
-
-    apply(yb)
-    copies = exchange(1)
-    ya2[...] = 0.5 * acc2[...] - 0.75 * yb2[...] - ya2[...]
-    for copy in copies:
-        copy.wait()
-    faces(1, ya, ya2, 0.5)
-
-    apply(ya)
-    copies = exchange(2)
-    yb2[...] = 0.5 * acc2[...] - 0.75 * ya2[...] - yb2[...]
-    for copy in copies:
-        copy.wait()
-    faces(2, yb, yb2, 0.5)
-    for h in range(2):
+        apply(ya, h)
+        stages.append(exchange(0, h))
+    for h in range(2):
+        yb2[h] = 0.25 * acc2[h] - 0.375 * ya2[h]
+    for h in range(2):
+        wait(stages[h])
+        faces(0, h, yb, yb2, 0.25)
+        apply(yb, h)
+        stages[h] = exchange(1, h)
+    for h in range(2):
+        ya2[h] = 0.5 * acc2[h] - 0.75 * yb2[h] - ya2[h]
+    for h in range(2):
+        wait(stages[h])
+        faces(1, h, ya, ya2, 0.5)
+        apply(ya, h)
+        stages[h] = exchange(2, h)
+    for h in range(2):
+        yb2[h] = 0.5 * acc2[h] - 0.75 * ya2[h] - yb2[h]
+
+    def pair(h):
+        high = both[:, 128 * h : 128 * h + 128]
+        low = both[:, NB + 128 * h : NB + 128 * h + 128]
+        return high, low, jnp.concatenate([high, low], axis=1)
+
+    def diagonal(h):
+        high, _, pairs = pair(h)
+        total = dot_tn(high, pairs)
+        cross = total[:, 128:]
+        return total[:, 0:128] + (cross + cross.T)
+
+    for h in range(2):
+        wait(stages[h])
+        faces(2, h, yb, yb2, 0.5)
         yb2[h, line(0, 15, 15), :] = jnp.zeros((195, 128), F32)
-
-    for h in range(2):
         y = yb2[h, 208:3120, :]
         top = y.astype(BF16)
         both[:, 128 * h : 128 * h + 128] = top
         both[:, NB + 128 * h : NB + 128 * h + 128] = (y - top.astype(F32)).astype(BF16)
+        block = diagonal(h)
+        if h == 0:
+            grams = [block]
+        else:
+            total = dot_tn(both[:, 0:128], pair(1)[2])
+            cross = dot_tn(both[:, NB : NB + 128], both[:, 128:NB])
+            grams += [total[:, 0:128] + (total[:, 128:] + cross), block]
     keep = pltpu.make_async_copy(both, yout, ysem)
     keep.start()
-    total = dot_tn(both[:, 0:NB], both[...])
-    cross = total[:, NB:]
-    gl[...] = (total[:, 0:NB] + (cross + cross.T)).reshape(8, 32, NB)
+    gl[...] = jnp.concatenate(grams, axis=0).reshape(8, 48, 128)
 
     copies = []
     for d in range(1, ndx):
@@ -235,7 +257,7 @@
     for d in range(1, ndx):
         chunk += ra[lax.rem(dx + d, ndx)]
     for p in range(16):
-        sb[p] = chunk[p // 2 * 4 : p // 2 * 4 + 4, p % 2 * 128 : p % 2 * 128 + 128]
+        sb[p] = chunk[3 * p : 3 * p + 3]
     copies = []
     for d in range(1, ndy):
         peer = lax.rem(dy + d, ndy)
@@ -253,14 +275,18 @@
     for copy in copies:
         copy.wait()
     for p in range(16):
-        gf[dx, p // 2 * 4 : p // 2 * 4 + 4, p % 2 * 128 : p % 2 * 128 + 128] = gb[p]
+        gf[dx, 3 * p : 3 * p + 3] = gb[p]
     copies = []
     for d in range(1, ndx):
         peer = lax.rem(dx + d, ndx)
         copies.append(remote(gf.at[dx], gf.at[dx], ds_.at[d], dr_.at[d], (peer, dy)))
     for copy in copies:
         copy.wait()
-    gout[...] = gf[...].reshape(NB, NB)
+    grams = gf[...].reshape(384, 128)
+    gout[0:128, 0:128] = grams[0:128]
+    gout[0:128, 128:NB] = grams[128:NB]
+    gout[128:NB, 0:128] = jnp.zeros((128, 128), F32)
+    gout[128:NB, 128:NB] = grams[NB:384]
     keep.wait()
 
 
@@ -394,7 +420,7 @@
                 pltpu.VMEM((2, 3120, 128), F32),
                 pltpu.VMEM((2, 3120, 128), F32),
                 pltpu.VMEM((2912, 2 * NB), BF16),
-                pltpu.VMEM((13, 14, NB), BF16),
+                pltpu.VMEM((2, 13, 14, 128), BF16),
                 pltpu.VMEM((2, 182, 128), BF16),
                 pltpu.VMEM((2, 13, 128), BF16),
                 pltpu.VMEM((2, 182, 128), BF16),
@@ -409,18 +435,18 @@
                 pltpu.VMEM((2, 2, 195, 128), BF16),
                 pltpu.VMEM((3, 2, 195, 128), BF16),
                 pltpu.VMEM((3, 4, 2, 13, 128), BF16),
-                pltpu.VMEM((8, 32, NB), F32),
-                pltpu.VMEM((8, 32, NB), F32),
-                pltpu.VMEM((16, 4, 128), F32),
-                pltpu.VMEM((16, 4, 128), F32),
-                pltpu.VMEM((16, 4, 128), F32),
-                pltpu.VMEM((8, 32, NB), F32),
+                pltpu.VMEM((8, 48, 128), F32),
+                pltpu.VMEM((8, 48, 128), F32),
+                pltpu.VMEM((16, 3, 128), F32),
+                pltpu.VMEM((16, 3, 128), F32),
+                pltpu.VMEM((16, 3, 128), F32),
+                pltpu.VMEM((8, 48, 128), F32),
                 dma((8,)),
                 dma,
-                dma((3,)),
-                dma((3,)),
-                dma((3, 9)),
-                dma((3, 9)),
+                dma((2, 3)),
+                dma((2, 3)),
+                dma((3, 2, 8)),
+                dma((3, 2, 8)),
                 dma((8,)),
                 dma((8,)),
                 dma((16,)),

time: 73.8 us -> 70.6 us (0.957)
  Pallas kernels: 73.4 us -> 70.3 us
    pallas_call x1, Pallas kernels: 60.9 us -> 57.7 us  [shards(): pl.pallas_call(lambda *refs: filter_kernel(ndx, ndy, *refs), out_shape=(j...]
where the time goes in v3:
time: 70.6 us; the launch traced here: 70.4 us
  Pallas kernels  70.3 us (100%)
    pallas_call x1, Pallas kernels, shards(): pl.pallas_call(lambda *refs: filter_kernel(ndx, ndy, *refs), out_shape=(j...  57.7 us
    pallas_call x1, Pallas kernels, shards(): pl.pallas_call(lambda *refs: basis_kernel(scale, *refs), out_shape=jax.Sh...  12.5 us

profile of v3, /device:TPU:1, one launch (start us, length us, event | category | flops | bytes accessed | tf_op | source)
XLA Modules:
  0.0 70.4 jit_solution(1590846084163969135)
XLA Ops:
  0.0 57.7 %filter.1 = (bf16[2912,512]{1,0:T(8,128)(2,1)}, f32[256,256]{1,0:T(8,128)}) custom-call(bf16[14,13,14,256]{3,2,1,0:T(8,128)(2,1)} %bitcast.2, bf16[2,2,2,512,512]{4,3,2,1,0:T(8,128)(2,1)} %refs_1_.1, s32[2,2,2,512]{3,2,1,0:T(2,128)} %refs_2_.1), custom_call_target="tpu_custom_call" | custom-call | tf_op jit(solution)/shard_map/filter/pallas_call | solution.py:405
  57.7 12.5 %basis.1 = f32[14,13,14,256]{3,2,1,0:T(8,128)} custom-call(bf16[2912,512]{1,0:T(8,128)(2,1)} %get-tuple-element.7.refs_0_, f32[256,256]{1,0:T(8,128)} %get-tuple-element.8.refs_1_), custom_call_target="tpu_custom_call" | custom-call | tf_op jit(solution)/shard_map/basis/pallas_call | solution.py:462

commit v4 on v3

--- a/solution.py
+++ b/solution.py
@@ -35,10 +35,10 @@
     ndx, ndy,
     orb, mats, conn,
     yout, gout,
-    abuf, ap, rmap, st, tt, ya2, yb2, acc2, both,
+    obuf, abuf, ap, rmap, st, tt, ya2, yb2, acc2, both,
     hx, hy, hc, shy, shc, sxl, sxh, syl, syh, scs, rxl, rxh, ryl, ryh, rcs,
     gl, ra, sb, rb, gb, gf,
-    msem, ysem, hss, hrs, ess, ers, as_, ar_, bs_, br_, cs_, cr_, ds_, dr_,
+    osem, msem, ysem, hss, hrs, ess, ers, as_, ar_, bs_, br_, cs_, cr_, ds_, dr_,
 ):
     dx = lax.axis_index("dx")
     dy = lax.axis_index("dy")
@@ -53,6 +53,8 @@
     for partner in partners:
         pl.semaphore_signal(barrier, inc=1, device_id=partner, device_id_type=MESH)
 
+    first_load = pltpu.make_async_copy(orb, obuf, osem)
+    first_load.start()
     loads = []
     for e in range(8):
         copy = pltpu.make_async_copy(mats.at[e // 4, e // 2 % 2, e % 2], abuf.at[e], msem.at[e])
@@ -65,18 +67,22 @@
         b_of = jnp.where(s_of < 7 - ey, s_of + 1 + ey, s_of - 7 + ey)
         rmap[ey] = (a_of * 225 + b_of * 15 + l_of).reshape(448, 128)
 
-    ya2[...] = jnp.zeros_like(ya2)
+    def line(i, slot, count):
+        return pl.ds(i * 208 + slot, 13 * count, stride=16)
+
+    for h in range(2):
+        ya2[h, 0:208, :] = jnp.zeros((208, 128), F32)
+        ya2[h, line(1, 14, 14), :] = jnp.zeros((182, 128), F32)
+        ya2[h, line(1, 15, 14), :] = jnp.zeros((182, 128), F32)
+    first_load.wait()
 
     def fill(i, carry):
-        plane = orb[i].astype(F32)
+        plane = obuf[i].astype(F32)
         for h in range(2):
             ya[h, i + 1, :, 0:14, :] = plane[:, :, 128 * h : 128 * h + 128]
         return carry
 
     lax.fori_loop(0, 14, fill, 0)
-
-    def line(i, slot, count):
-        return pl.ds(i * 208 + slot, 13 * count, stride=16)
 
     for h in range(2):
         shy[h] = ya2[h, line(1, 13, 14), :].astype(BF16)
@@ -102,21 +108,48 @@
         copy.start()
         return copy
 
-    fold(0)
+    x_low, x_high, y_low, y_high = dx > 0, dx < ndx - 1, dy > 0, dy < ndy - 1
+
+    def toward(src, dst, ssem, rsem, sx, sy):
+        where = (dx + sx, dy + sy)
+        copy = pltpu.make_async_remote_copy(
+            src_ref=src, dst_ref=dst, send_sem=ssem, recv_sem=rsem, device_id=where, device_id_type=MESH
+        )
+        ahead = [f for f in ({1: x_high, -1: x_low}.get(sx), {1: y_high, -1: y_low}.get(sy)) if f is not None]
+        behind = [f for f in ({1: x_low, -1: x_high}.get(sx), {1: y_low, -1: y_high}.get(sy)) if f is not None]
+        ahead = ahead[0] if len(ahead) == 1 else jnp.logical_and(*ahead)
+        behind = behind[0] if len(behind) == 1 else jnp.logical_and(*behind)
+
+        @pl.when(ahead)
+        def _():
+            copy.start()
+
+        return copy, ahead, behind
+
+    def wait(copies):
+        for copy, ahead, behind in copies:
+
+            @pl.when(behind)
+            def _():
+                copy.wait_recv()
+
+            @pl.when(ahead)
+            def _():
+                copy.wait_send()
+
     pl.semaphore_wait(barrier, len(partners))
     halo = []
     for h in range(2):
-        half = orb.at[13, :, :, 128 * h : 128 * h + 128]
+        half = obuf.at[13, :, :, 128 * h : 128 * h + 128]
         halo.append(
             [
-                remote(shy.at[h], hy.at[h], hss.at[h, 1], hrs.at[h, 1], (dx, yp)),
-                remote(half, hx.at[h], hss.at[h, 0], hrs.at[h, 0], (xp, dy)),
-                remote(shc.at[h], hc.at[h], hss.at[h, 2], hrs.at[h, 2], (xp, yp)),
+                toward(shc.at[h], hc.at[h], hss.at[h, 2], hrs.at[h, 2], 1, 1),
+                toward(shy.at[h], hy.at[h], hss.at[h, 1], hrs.at[h, 1], 0, 1),
+                toward(half, hx.at[h], hss.at[h, 0], hrs.at[h, 0], 1, 0),
             ]
         )
-    for c in range(1, 4):
+    for c in range(4):
         fold(c)
-    x_low, x_high, y_low, y_high = dx > 0, dx < ndx - 1, dy > 0, dy < ndy - 1
 
     sub = lax.broadcasted_iota(jnp.int32, (8, 7, 8, 128), 2)
 
@@ -147,23 +180,27 @@
     def exchange(t, h):
         copies = []
 
-        def send(n, src, dst, where):
-            copies.append(remote(src, dst, ess.at[t, h, n], ers.at[t, h, n], where))
-
+        def send(n, src, dst, sx, sy):
+            copies.append(toward(src, dst, ess.at[t, h, n], ers.at[t, h, n], sx, sy))
+
+        corners = [(0, 15, -1, -1), (14, 13, 1, 1), (0, 13, -1, 1), (14, 15, 1, -1)]
+        count = 4 if t < 2 else 1
+        for n, (i, slot, _, _) in enumerate(corners[:count]):
+            scs[t, n, h] = acc2[h, line(i, slot, 1), :].astype(BF16)
         syl[t, h] = acc2[h, line(0, 15, 15), :].astype(BF16)
-        send(0, syl.at[t, h], ryh.at[t, h], (dx, ym))
         if t < 2:
             syh[t, h] = acc2[h, line(0, 13, 15), :].astype(BF16)
-            send(1, syh.at[t, h], ryl.at[t, h], (dx, yp))
         sxl[t, h] = acc[h, 0].astype(BF16)
-        send(2, sxl.at[t, h], rxh.at[t, h], (xm, dy))
         if t < 2:
             sxh[t, h] = acc[h, 14].astype(BF16)
-            send(3, sxh.at[t, h], rxl.at[t, h], (xp, dy))
-        corners = [(0, 15, (xm, ym)), (14, 13, (xp, yp)), (0, 13, (xm, yp)), (14, 15, (xp, ym))]
-        for n, (i, slot, where) in enumerate(corners[: 4 if t < 2 else 1]):
-            scs[t, n, h] = acc2[h, line(i, slot, 1), :].astype(BF16)
-            send(4 + n, scs.at[t, n, h], rcs.at[t, n, h], where)
+        for n, (_, _, sx, sy) in enumerate(corners[:count]):
+            send(4 + n, scs.at[t, n, h], rcs.at[t, n, h], sx, sy)
+        send(0, syl.at[t, h], ryh.at[t, h], 0, -1)
+        if t < 2:
+            send(1, syh.at[t, h], ryl.at[t, h], 0, 1)
+        send(2, sxl.at[t, h], rxh.at[t, h], -1, 0)
+        if t < 2:
+            send(3, sxh.at[t, h], rxl.at[t, h], 1, 0)
         return copies
 
     def gated(flag, value, coef):
@@ -185,10 +222,6 @@
             y[h, 0] = jnp.where(x_low, y[h, 0], 0.0)
             edge = y2[h, line(0, 15, 15), :]
             y2[h, line(0, 15, 15), :] = jnp.where(y_low, edge, 0.0)
-
-    def wait(copies):
-        for copy in copies:
-            copy.wait()
 
     stages = []
     for h in range(2):
@@ -408,9 +441,10 @@
                 jax.ShapeDtypeStruct((2912, 2 * NB), BF16),
                 jax.ShapeDtypeStruct((NB, NB), F32),
             ),
-            in_specs=[vmem, anywhere, vmem],
+            in_specs=[anywhere, anywhere, vmem],
             out_specs=(anywhere, vmem),
             scratch_shapes=[
+                pltpu.VMEM((14, 13, 14, NB), BF16),
                 pltpu.VMEM((8, 512, 512), BF16),
                 pltpu.VMEM((8, 448, 448), BF16),
                 pltpu.VMEM((2, 448, 128), jnp.int32),
@@ -441,6 +475,7 @@
                 pltpu.VMEM((16, 3, 128), F32),
                 pltpu.VMEM((16, 3, 128), F32),
                 pltpu.VMEM((8, 48, 128), F32),
+                dma,
                 dma((8,)),
                 dma,
                 dma((2, 3)),

time: 70.6 us -> 68.5 us (0.970)
  Pallas kernels: 70.3 us -> 68.1 us
    pallas_call x1, Pallas kernels: 57.7 us -> 55.5 us  [shards(): pl.pallas_call(lambda *refs: filter_kernel(ndx, ndy, *refs), out_shape=(j...]
where the time goes in v4:
time: 68.5 us; the launch traced here: 68.2 us
  Pallas kernels  68.1 us (99%)
    pallas_call x1, Pallas kernels, shards(): pl.pallas_call(lambda *refs: filter_kernel(ndx, ndy, *refs), out_shape=(j...  55.5 us
    pallas_call x1, Pallas kernels, shards(): pl.pallas_call(lambda *refs: basis_kernel(scale, *refs), out_shape=jax.Sh...  12.5 us

profile of v4, /device:TPU:1, one launch (start us, length us, event | category | flops | bytes accessed | tf_op | source)
XLA Modules:
  0.0 68.2 jit_solution(8155875872828878768)
XLA Ops:
  0.0 55.5 %filter.1 = (bf16[2912,512]{1,0:T(8,128)(2,1)}, f32[256,256]{1,0:T(8,128)}) custom-call(bf16[14,13,14,256]{3,2,1,0:T(8,128)(2,1)} %bitcast.2, bf16[2,2,2,512,512]{4,3,2,1,0:T(8,128)(2,1)} %refs_1_.1, s32[2,2,2,512]{3,2,1,0:T(2,128)} %refs_2_.1), custom_call_target="tpu_custom_call" | custom-call | tf_op jit(solution)/shard_map/filter/pallas_call | solution.py:438
  55.6 12.5 %basis.1 = f32[14,13,14,256]{3,2,1,0:T(8,128)} custom-call(bf16[2912,512]{1,0:T(8,128)(2,1)} %get-tuple-element.7.refs_0_, f32[256,256]{1,0:T(8,128)} %get-tuple-element.8.refs_1_), custom_call_target="tpu_custom_call" | custom-call | tf_op jit(solution)/shard_map/basis/pallas_call | solution.py:497

commit v5 on v4

--- a/solution.py
+++ b/solution.py
@@ -32,12 +32,12 @@
 
 
 def filter_kernel(
-    ndx, ndy,
+    ndx, ndy, scale,
     orb, mats, conn,
-    yout, gout,
+    yout, wout,
     obuf, abuf, ap, rmap, st, tt, ya2, yb2, acc2, both,
     hx, hy, hc, shy, shc, sxl, sxh, syl, syh, scs, rxl, rxh, ryl, ryh, rcs,
-    gl, ra, sb, rb, gb, gf,
+    gl0, ra0, gf0, gl1, ra1, gf1, sb0, rb0, gb0, sb1, rb1, gb1, work, pivots,
     osem, msem, ysem, hss, hrs, ess, ers, as_, ar_, bs_, br_, cs_, cr_, ds_, dr_,
 ):
     dx = lax.axis_index("dx")
@@ -137,6 +137,7 @@
             def _():
                 copy.wait_send()
 
+    fold(0)
     pl.semaphore_wait(barrier, len(partners))
     halo = []
     for h in range(2):
@@ -148,7 +149,7 @@
                 toward(half, hx.at[h], hss.at[h, 0], hrs.at[h, 0], 1, 0),
             ]
         )
-    for c in range(4):
+    for c in range(1, 4):
         fold(c)
 
     sub = lax.broadcasted_iota(jnp.int32, (8, 7, 8, 128), 2)
@@ -261,7 +262,7 @@
         cross = total[:, 128:]
         return total[:, 0:128] + (cross + cross.T)
 
-    for h in range(2):
+    def finish(h):
         wait(stages[h])
         faces(2, h, yb, yb2, 0.5)
         yb2[h, line(0, 15, 15), :] = jnp.zeros((195, 128), F32)
@@ -269,57 +270,89 @@
         top = y.astype(BF16)
         both[:, 128 * h : 128 * h + 128] = top
         both[:, NB + 128 * h : NB + 128 * h + 128] = (y - top.astype(F32)).astype(BF16)
-        block = diagonal(h)
-        if h == 0:
-            grams = [block]
-        else:
-            total = dot_tn(both[:, 0:128], pair(1)[2])
-            cross = dot_tn(both[:, NB : NB + 128], both[:, 128:NB])
-            grams += [total[:, 0:128] + (total[:, 128:] + cross), block]
+
+    def members(me, count):
+        return [(d, lax.rem(me + d, count)) for d in range(1, count)]
+
+    def settle(copies):
+        for copy in copies:
+            copy.wait()
+
+    def scatter_x(gl, ra, n):
+        return [
+            remote(gl.at[p], ra.at[dx], as_.at[n, d], ar_.at[n, d], (p, dy)) for d, p in members(dx, ndx)
+        ]
+
+    def scatter_y(gl, ra, sb, rb, n):
+        chunk = gl[dx]
+        for _, p in members(dx, ndx):
+            chunk += ra[p]
+        for p in range(16):
+            sb[p] = chunk[(n + 1) * p : (n + 1) * p + n + 1]
+        return [
+            remote(sb.at[p], rb.at[dy], bs_.at[n, d], br_.at[n, d], (dx, p)) for d, p in members(dy, ndy)
+        ]
+
+    def gather_y(sb, rb, gb, n):
+        piece = sb[dy]
+        for _, p in members(dy, ndy):
+            piece += rb[p]
+        gb[dy] = piece
+        return [
+            remote(gb.at[dy], gb.at[dy], cs_.at[n, d], cr_.at[n, d], (dx, p)) for d, p in members(dy, ndy)
+        ]
+
+    def gather_x(gb, gf, n):
+        for p in range(16):
+            gf[dx, (n + 1) * p : (n + 1) * p + n + 1] = gb[p]
+        return [
+            remote(gf.at[dx], gf.at[dx], ds_.at[n, d], dr_.at[n, d], (p, dy)) for d, p in members(dx, ndx)
+        ]
+
+    finish(0)
+    gl0[...] = diagonal(0).reshape(8, 16, 128)
+    round0 = scatter_x(gl0, ra0, 0)
+    finish(1)
     keep = pltpu.make_async_copy(both, yout, ysem)
     keep.start()
-    gl[...] = jnp.concatenate(grams, axis=0).reshape(8, 48, 128)
-
-    copies = []
-    for d in range(1, ndx):
-        peer = lax.rem(dx + d, ndx)
-        copies.append(remote(gl.at[peer], ra.at[dx], as_.at[d], ar_.at[d], (peer, dy)))
-    for copy in copies:
-        copy.wait()
-    chunk = gl[dx]
-    for d in range(1, ndx):
-        chunk += ra[lax.rem(dx + d, ndx)]
-    for p in range(16):
-        sb[p] = chunk[3 * p : 3 * p + 3]
-    copies = []
-    for d in range(1, ndy):
-        peer = lax.rem(dy + d, ndy)
-        copies.append(remote(sb.at[peer], rb.at[dy], bs_.at[d], br_.at[d], (dx, peer)))
-    for copy in copies:
-        copy.wait()
-    piece = sb[dy]
-    for d in range(1, ndy):
-        piece += rb[lax.rem(dy + d, ndy)]
-    gb[dy] = piece
-    copies = []
-    for d in range(1, ndy):
-        peer = lax.rem(dy + d, ndy)
-        copies.append(remote(gb.at[dy], gb.at[dy], cs_.at[d], cr_.at[d], (dx, peer)))
-    for copy in copies:
-        copy.wait()
-    for p in range(16):
-        gf[dx, 3 * p : 3 * p + 3] = gb[p]
-    copies = []
-    for d in range(1, ndx):
-        peer = lax.rem(dx + d, ndx)
-        copies.append(remote(gf.at[dx], gf.at[dx], ds_.at[d], dr_.at[d], (peer, dy)))
-    for copy in copies:
-        copy.wait()
-    grams = gf[...].reshape(384, 128)
-    gout[0:128, 0:128] = grams[0:128]
-    gout[0:128, 128:NB] = grams[128:NB]
-    gout[128:NB, 0:128] = jnp.zeros((128, 128), F32)
-    gout[128:NB, 128:NB] = grams[NB:384]
+    total = dot_tn(both[:, 0:128], pair(1)[2])
+    cross = dot_tn(both[:, NB : NB + 128], both[:, 128:NB])
+    gl1[0:4] = (total[:, 0:128] + (total[:, 128:] + cross)).reshape(4, 32, 128)
+    gl1[4:8] = diagonal(1).reshape(4, 32, 128)
+    round1 = scatter_x(gl1, ra1, 1)
+    settle(round0)
+    round0 = scatter_y(gl0, ra0, sb0, rb0, 0)
+    settle(round1)
+    round1 = scatter_y(gl1, ra1, sb1, rb1, 1)
+    settle(round0)
+    round0 = gather_y(sb0, rb0, gb0, 0)
+    settle(round1)
+    round1 = gather_y(sb1, rb1, gb1, 1)
+    settle(round0)
+    round0 = gather_x(gb0, gf0, 0)
+    settle(round1)
+    round1 = gather_x(gb1, gf1, 1)
+
+    def put(block, rows, cols):
+        block = block * scale
+        top = block.astype(BF16)
+        low = (block - top.astype(F32)).astype(BF16)
+        for start, value in ((0, top), (NB, top), (2 * NB, low)):
+            wout[rows, start + cols : start + cols + 128] = value
+
+    settle(round0)
+    work[...] = gf0[...].reshape(128, 128)
+    w1 = factor_inverse(work, pivots)
+    put(w1, slice(0, 128), 0)
+    put(jnp.zeros((128, 128), F32), slice(0, 128), 128)
+    settle(round1)
+    rows01 = gf1[0:4].reshape(128, 128)
+    upper = exact(w1, rows01, 1)
+    work[...] = gf1[4:8].reshape(128, 128) - exact(upper, upper, 0)
+    mid = exact(upper, w1, 0)
+    w2 = factor_inverse(work, pivots)
+    put(w2, slice(128, NB), 128)
+    put(-exact(w2, mid, 1), slice(128, NB), 0)
     keep.wait()
 
 
@@ -330,30 +363,32 @@
     return a, b, (rest - b.astype(F32)).astype(BF16)
 
 
-def factor_inverse(g, work):
+def exact(left, right, dim):
+    l1, l2, l3 = split3(left)
+    r1, r2, r3 = split3(right)
+    left = jnp.concatenate([l1, l1, l1, l2, l2, l3], axis=dim)
+    right = jnp.concatenate([r1, r2, r3, r1, r2, r1], axis=0)
+    return lax.dot_general(left, right, (((dim,), (0,)), ((), ())), preferred_element_type=F32)
+
+
+def factor_inverse(work, pivots):
     rows = lax.broadcasted_iota(jnp.int32, (8, 128), 0)
     lanes = lax.broadcasted_iota(jnp.int32, (8, 128), 1)
-    scales = []
-    for o in range(8):
-        base = 32 * o
-        source = g if o == 0 else work
-        tiles = [
-            [source[base + 8 * t : base + 8 * t + 8, 128 * h : 128 * h + 128] for h in range(2)]
-            for t in range(4)
-        ]
+
+    def step(o, carry):
+        tiles = [work[8 * t : 8 * t + 8, :] for t in range(4)]
         factors = []
-        half = base // 128
         for s in range(4):
-            first = base + 8 * s - 128 * half
+            first = 8 * s
             inside = jnp.logical_and(lanes >= first, lanes < first + 8)
             columns = []
             for q in range(s, 4):
-                tile = tiles[q][half]
+                tile = tiles[q]
                 columns.append(
                     [jnp.broadcast_to(tile[:, first + j : first + j + 1], (8, 128)) for j in range(8)]
                 )
                 fresh = jnp.where(lanes == rows + first, 1.0, 0.0) if q == s else 0.0
-                tiles[q][half] = jnp.where(inside, fresh, tile)
+                tiles[q] = jnp.where(inside, fresh, tile)
             scale = jnp.ones((8, 128), F32)
             factor = jnp.ones((8, 128), F32)
             for k in range(8):
@@ -361,7 +396,7 @@
                 inv = 1.0 / lead[0]
                 scale = jnp.where(rows == k, lead[0], scale)
                 factor = jnp.where(rows == k, inv, factor)
-                pivot = [jnp.broadcast_to(tiles[s][h][k : k + 1, :], (8, 128)) * inv for h in range(2)]
+                pivot = jnp.broadcast_to(tiles[s][k : k + 1, :], (8, 128)) * inv
                 lead = [v * inv for v in lead]
                 for q in range(s, 4):
                     if q == s and k == 7:
@@ -371,54 +406,40 @@
                         column = jnp.where(rows > k, column, 0.0)
                     for j in range(k + 1, 8):
                         columns[q - s][j] = columns[q - s][j] - column * lead[j - k]
-                    for h in range(2):
-                        tiles[q][h] = tiles[q][h] - column * pivot[h]
-            scales.append(lax.rsqrt(scale))
+                    tiles[q] = tiles[q] - column * pivot
+            pivots[pl.ds(32 * o + 8 * s, 8), :] = lax.rsqrt(scale)
             factors.append(factor)
-        for t in range(4):
-            for h in range(2):
-                work[base + 8 * t : base + 8 * t + 8, 128 * h : 128 * h + 128] = tiles[t][h]
-        if o < 7:
-            u = jnp.concatenate([jnp.concatenate(tiles[t], axis=1) for t in range(4)], axis=0)
-            f = jnp.concatenate([jnp.concatenate([v, v], axis=1) for v in factors], axis=0)
-            r = lax.broadcasted_iota(jnp.int32, (32, NB), 0) + base
-            c = lax.broadcasted_iota(jnp.int32, (32, NB), 1)
-            v = jnp.where(jnp.logical_and(c > r, c < base + 32), 0.0, u * f)
-            start = 128 * ((base + 32) // 128)
-            u1, u2, u3 = split3(u[:, start:])
-            v1, v2, v3 = split3(v)
-            left = jnp.concatenate([u1, u1, u1, u2, u2, u3], axis=0)
-            right = jnp.concatenate([v1, v2, v3, v1, v2, v1], axis=0)
-            change = lax.dot_general(
-                left, right, (((0,), (0,)), ((), ())), preferred_element_type=F32
-            )
-            rest = slice(base + 32, NB)
-            old = (g if o == 0 else work)[rest, :]
-            cc = lax.broadcasted_iota(jnp.int32, old.shape, 1)
-            old = jnp.where(jnp.logical_and(cc >= base, cc < base + 32), 0.0, old)
-            work[rest, :] = old - change[base + 32 - start :, :]
-    for t in range(32):
-        for h in range(2):
-            tile = work[8 * t : 8 * t + 8, 128 * h : 128 * h + 128] * scales[t]
-            work[8 * t : 8 * t + 8, 128 * h : 128 * h + 128] = jnp.where(
-                lanes + 128 * h <= rows + 8 * t, tile, 0.0
-            )
-
-
-def basis_kernel(scale, y, g, out, ybuf, stage, work, whh, wlo, yin, osem):
-    load = pltpu.make_async_copy(y, ybuf, yin)
-    load.start()
-    factor_inverse(g, work)
-    w = work[...] * scale
-    top = w.astype(BF16)
-    whh[:, 0:NB] = top
-    whh[:, NB:] = top
-    wlo[...] = (w - top.astype(F32)).astype(BF16)
-    load.wait()
+        u = jnp.concatenate(tiles, axis=0)
+        r = lax.broadcasted_iota(jnp.int32, (32, 128), 0)
+        c = lax.broadcasted_iota(jnp.int32, (32, 128), 1)
+        v = jnp.where(jnp.logical_and(c > r, c < 32), 0.0, u * jnp.concatenate(factors, axis=0))
+        change = exact(u, v, 0)
+        old = work[32:128, :]
+        r = lax.broadcasted_iota(jnp.int32, (96, 128), 0)
+        c = lax.broadcasted_iota(jnp.int32, (96, 128), 1)
+        fresh = jnp.where(c < 32, 0.0, old) - change[32:128, :]
+        work[0:96, :] = pltpu.roll(jnp.where(r < 96 - 32 * o, fresh, old), 96, 1)
+        work[96:128, :] = pltpu.roll(u, 96, 1)
+        return carry
+
+    lax.fori_loop(0, 4, step, 0)
+    r = lax.broadcasted_iota(jnp.int32, (128, 128), 0)
+    c = lax.broadcasted_iota(jnp.int32, (128, 128), 1)
+    return jnp.where(c <= r, work[...] * pivots[...], 0.0)
+
+
+def basis_kernel(y, w, out, ybuf, stage, yin, osem):
+    loads = []
+    for i in range(14):
+        rows = pl.ds(208 * i, 208)
+        load = pltpu.make_async_copy(y.at[rows], ybuf.at[rows], yin.at[i])
+        load.start()
+        loads.append(load)
     copies = []
     for i in range(14):
+        loads[i].wait()
         rows = slice(208 * i, 208 * i + 208)
-        q = dot_nt(ybuf[rows, :], whh[...]) + dot_nt(ybuf[rows, 0:NB], wlo[...])
+        q = dot_nt(ybuf[rows, :], w[:, 0 : 2 * NB]) + dot_nt(ybuf[rows, 0:NB], w[:, 2 * NB :])
         stage[i] = q.reshape(13, 16, NB)[:, 0:14, :]
         copy = pltpu.make_async_copy(stage.at[i], out.at[i], osem.at[i])
         copy.start()
@@ -435,11 +456,11 @@
 
     def shards(orbitals, elem_mats, conn):
         dma = pltpu.SemaphoreType.DMA
-        y, g = pl.pallas_call(
-            lambda *refs: filter_kernel(ndx, ndy, *refs),
+        y, w = pl.pallas_call(
+            lambda *refs: filter_kernel(ndx, ndy, scale, *refs),
             out_shape=(
                 jax.ShapeDtypeStruct((2912, 2 * NB), BF16),
-                jax.ShapeDtypeStruct((NB, NB), F32),
+                jax.ShapeDtypeStruct((NB, 3 * NB), BF16),
             ),
             in_specs=[anywhere, anywhere, vmem],
             out_specs=(anywhere, vmem),
@@ -469,12 +490,20 @@
                 pltpu.VMEM((2, 2, 195, 128), BF16),
                 pltpu.VMEM((3, 2, 195, 128), BF16),
                 pltpu.VMEM((3, 4, 2, 13, 128), BF16),
-                pltpu.VMEM((8, 48, 128), F32),
-                pltpu.VMEM((8, 48, 128), F32),
-                pltpu.VMEM((16, 3, 128), F32),
-                pltpu.VMEM((16, 3, 128), F32),
-                pltpu.VMEM((16, 3, 128), F32),
-                pltpu.VMEM((8, 48, 128), F32),
+                pltpu.VMEM((8, 16, 128), F32),
+                pltpu.VMEM((8, 16, 128), F32),
+                pltpu.VMEM((8, 16, 128), F32),
+                pltpu.VMEM((8, 32, 128), F32),
+                pltpu.VMEM((8, 32, 128), F32),
+                pltpu.VMEM((8, 32, 128), F32),
+                pltpu.VMEM((16, 1, 128), F32),
+                pltpu.VMEM((16, 1, 128), F32),
+                pltpu.VMEM((16, 1, 128), F32),
+                pltpu.VMEM((16, 2, 128), F32),
+                pltpu.VMEM((16, 2, 128), F32),
+                pltpu.VMEM((16, 2, 128), F32),
+                pltpu.VMEM((128, 128), F32),
+                pltpu.VMEM((128, 128), F32),
                 dma,
                 dma((8,)),
                 dma,
@@ -482,34 +511,31 @@
                 dma((2, 3)),
                 dma((3, 2, 8)),
                 dma((3, 2, 8)),
-                dma((8,)),
-                dma((8,)),
-                dma((16,)),
-                dma((16,)),
-                dma((16,)),
-                dma((16,)),
-                dma((8,)),
-                dma((8,)),
+                dma((2, 8)),
+                dma((2, 8)),
+                dma((2, 16)),
+                dma((2, 16)),
+                dma((2, 16)),
+                dma((2, 16)),
+                dma((2, 8)),
+                dma((2, 8)),
             ],
             compiler_params=pltpu.CompilerParams(collective_id=0, has_side_effects=True),
             name="filter",
         )(jnp.swapaxes(orbitals, 1, 2), elem_mats, conn)
         filtered = pl.pallas_call(
-            lambda *refs: basis_kernel(scale, *refs),
+            basis_kernel,
             out_shape=jax.ShapeDtypeStruct((14, 13, 14, NB), F32),
             in_specs=[anywhere, vmem],
             out_specs=anywhere,
             scratch_shapes=[
                 pltpu.VMEM((2912, 2 * NB), BF16),
                 pltpu.VMEM((14, 13, 14, NB), F32),
-                pltpu.VMEM((NB, NB), F32),
-                pltpu.VMEM((NB, 2 * NB), BF16),
-                pltpu.VMEM((NB, NB), BF16),
-                dma,
+                dma((14,)),
                 dma((14,)),
             ],
             name="basis",
-        )(y, g)
+        )(y, w)
         return jnp.swapaxes(filtered, 1, 2)
 
     in_specs = (

time: 68.5 us -> 71 us (1.036)
  Pallas kernels: 68.1 us -> 70.7 us
    pallas_call x2, Pallas kernels: 68.1 us -> 70.7 us  [the longest x1 62.6 us: shards(): pl.pallas_call(lambda *refs: filter_kernel(ndx, ndy, scale, *refs), out_s...]
where the time goes in v5:
time: 71 us; the launch traced here: 70.8 us
  Pallas kernels  70.7 us (100%)
    pallas_call x1, Pallas kernels, shards(): pl.pallas_call(lambda *refs: filter_kernel(ndx, ndy, scale, *refs), out_s...  62.6 us
    pallas_call x1, Pallas kernels, shards(): pl.pallas_call(basis_kernel, out_shape=jax.ShapeDtypeStruct((14, 13, 14,...  8.07 us

profile of v5, /device:TPU:1, one launch (start us, length us, event | category | flops | bytes accessed | tf_op | source)
XLA Modules:
  0.0 70.8 jit_solution(1652830183918686489)
XLA Ops:
  0.0 62.6 %filter.1 = (bf16[2912,512]{1,0:T(8,128)(2,1)}, bf16[256,768]{1,0:T(8,128)(2,1)}) custom-call(bf16[14,13,14,256]{3,2,1,0:T(8,128)(2,1)} %bitcast.2, bf16[2,2,2,512,512]{4,3,2,1,0:T(8,128)(2,1)} %refs_1_.1, s32[2,2,2,512]{3,2,1,0:T(2,128)} %refs_2_.1), custom_call_target="tpu_custom_call" | custom-call | tf_op jit(solution)/shard_map/filter/pallas_call | solution.py:459
  62.6 8.1 %basis.1 = f32[14,13,14,256]{3,2,1,0:T(8,128)} custom-call(bf16[2912,512]{1,0:T(8,128)(2,1)} %get-tuple-element.7.y, bf16[256,768]{1,0:T(8,128)(2,1)} %get-tuple-element.8.w), custom_call_target="tpu_custom_call" | custom-call | tf_op jit(solution)/shard_map/basis/pallas_call | solution.py:526

commit v6 on v4

--- a/solution.py
+++ b/solution.py
@@ -137,6 +137,7 @@
             def _():
                 copy.wait_send()
 
+    fold(0)
     pl.semaphore_wait(barrier, len(partners))
     halo = []
     for h in range(2):
@@ -148,7 +149,7 @@
                 toward(half, hx.at[h], hss.at[h, 0], hrs.at[h, 0], 1, 0),
             ]
         )
-    for c in range(4):
+    for c in range(1, 4):
         fold(c)
 
     sub = lax.broadcasted_iota(jnp.int32, (8, 7, 8, 128), 2)
@@ -330,7 +331,9 @@
     return a, b, (rest - b.astype(F32)).astype(BF16)
 
 
-def factor_inverse(g, work):
+def factor_inverse(g, work, ones):
+    ones[...] = jnp.ones((8, 128), F32)
+    one = ones[...]
     rows = lax.broadcasted_iota(jnp.int32, (8, 128), 0)
     lanes = lax.broadcasted_iota(jnp.int32, (8, 128), 1)
     scales = []
@@ -350,7 +353,10 @@
             for q in range(s, 4):
                 tile = tiles[q][half]
                 columns.append(
-                    [jnp.broadcast_to(tile[:, first + j : first + j + 1], (8, 128)) for j in range(8)]
+                    [
+                        jnp.broadcast_to(tile[:, first + j : first + j + 1], (8, 128)) * one
+                        for j in range(8)
+                    ]
                 )
                 fresh = jnp.where(lanes == rows + first, 1.0, 0.0) if q == s else 0.0
                 tiles[q][half] = jnp.where(inside, fresh, tile)
@@ -362,7 +368,7 @@
                 scale = jnp.where(rows == k, lead[0], scale)
                 factor = jnp.where(rows == k, inv, factor)
                 pivot = [jnp.broadcast_to(tiles[s][h][k : k + 1, :], (8, 128)) * inv for h in range(2)]
-                lead = [v * inv for v in lead]
+                ready = [v * inv for v in lead]
                 for q in range(s, 4):
                     if q == s and k == 7:
                         continue
@@ -370,7 +376,11 @@
                     if q == s:
                         column = jnp.where(rows > k, column, 0.0)
                     for j in range(k + 1, 8):
-                        columns[q - s][j] = columns[q - s][j] - column * lead[j - k]
+                        if q == s:
+                            change = (column * lead[j - k]) * inv
+                        else:
+                            change = column * ready[j - k]
+                        columns[q - s][j] = columns[q - s][j] - change
                     for h in range(2):
                         tiles[q][h] = tiles[q][h] - column * pivot[h]
             scales.append(lax.rsqrt(scale))
@@ -405,22 +415,24 @@
             )
 
 
-def basis_kernel(scale, y, g, out, ybuf, stage, work, whh, wlo, yin, osem):
+def basis_kernel(scale, y, g, out, ybuf, stage, work, ones, weights, yin, osem):
     load = pltpu.make_async_copy(y, ybuf, yin)
     load.start()
-    factor_inverse(g, work)
-    w = work[...] * scale
+    factor_inverse(g, work, ones)
+    w = work[...].T * scale
     top = w.astype(BF16)
-    whh[:, 0:NB] = top
-    whh[:, NB:] = top
-    wlo[...] = (w - top.astype(F32)).astype(BF16)
+    weights[0:NB] = top
+    weights[NB : 2 * NB] = top
+    weights[2 * NB :] = (w - top.astype(F32)).astype(BF16)
     load.wait()
     copies = []
-    for i in range(14):
-        rows = slice(208 * i, 208 * i + 208)
-        q = dot_nt(ybuf[rows, :], whh[...]) + dot_nt(ybuf[rows, 0:NB], wlo[...])
-        stage[i] = q.reshape(13, 16, NB)[:, 0:14, :]
-        copy = pltpu.make_async_copy(stage.at[i], out.at[i], osem.at[i])
+    for start, count in ((0, 4), (4, 4), (8, 4), (12, 2)):
+        rows = slice(208 * start, 208 * (start + count))
+        left = jnp.concatenate([ybuf[rows, :], ybuf[rows, 0:NB]], axis=1)
+        q = dot_nn(left, weights[...]).reshape(count, 13, 16, NB)
+        planes = slice(start, start + count)
+        stage[planes] = q[:, :, 0:14, :]
+        copy = pltpu.make_async_copy(stage.at[planes], out.at[planes], osem.at[start])
         copy.start()
         copies.append(copy)
     for copy in copies:
@@ -503,8 +515,8 @@
                 pltpu.VMEM((2912, 2 * NB), BF16),
                 pltpu.VMEM((14, 13, 14, NB), F32),
                 pltpu.VMEM((NB, NB), F32),
-                pltpu.VMEM((NB, 2 * NB), BF16),
-                pltpu.VMEM((NB, NB), BF16),
+                pltpu.VMEM((8, 128), F32),
+                pltpu.VMEM((3 * NB, NB), BF16),
                 dma,
                 dma((14,)),
             ],

time: 68.5 us -> 65.2 us (0.952)
  Pallas kernels: 68.1 us -> 64.8 us
    pallas_call x1, Pallas kernels: 12.5 us -> 10.1 us  [shards(): pl.pallas_call(lambda *refs: basis_kernel(scale, *refs), out_shape=jax.Sh...]
    pallas_call x1, Pallas kernels: 55.5 us -> 54.7 us  [shards(): pl.pallas_call(lambda *refs: filter_kernel(ndx, ndy, *refs), out_shape=(j...]
where the time goes in v6:
time: 65.2 us; the launch traced here: 65 us
  Pallas kernels  64.8 us (99%)
    pallas_call x1, Pallas kernels, shards(): pl.pallas_call(lambda *refs: filter_kernel(ndx, ndy, *refs), out_shape=(j...  54.7 us
    pallas_call x1, Pallas kernels, shards(): pl.pallas_call(lambda *refs: basis_kernel(scale, *refs), out_shape=jax.Sh...  10.1 us

profile of v6, /device:TPU:1, one launch (start us, length us, event | category | flops | bytes accessed | tf_op | source)
XLA Modules:
  0.0 65.0 jit_solution(8779725815594138404)
XLA Ops:
  0.0 54.7 %filter.1 = (bf16[2912,512]{1,0:T(8,128)(2,1)}, f32[256,256]{1,0:T(8,128)}) custom-call(bf16[14,13,14,256]{3,2,1,0:T(8,128)(2,1)} %bitcast.2, bf16[2,2,2,512,512]{4,3,2,1,0:T(8,128)(2,1)} %refs_1_.1, s32[2,2,2,512]{3,2,1,0:T(2,128)} %refs_2_.1), custom_call_target="tpu_custom_call" | custom-call | tf_op jit(solution)/shard_map/filter/pallas_call | solution.py:450
  54.7 10.1 %basis.1 = f32[14,13,14,256]{3,2,1,0:T(8,128)} custom-call(bf16[2912,512]{1,0:T(8,128)(2,1)} %get-tuple-element.7.refs_0_, f32[256,256]{1,0:T(8,128)} %get-tuple-element.8.refs_1_), custom_call_target="tpu_custom_call" | custom-call | tf_op jit(solution)/shard_map/basis/pallas_call | solution.py:509

commit v7 on v6

--- a/solution.py
+++ b/solution.py
@@ -37,8 +37,8 @@
     yout, gout,
     obuf, abuf, ap, rmap, st, tt, ya2, yb2, acc2, both,
     hx, hy, hc, shy, shc, sxl, sxh, syl, syh, scs, rxl, rxh, ryl, ryh, rcs,
-    gl, ra, sb, rb, gb, gf,
-    osem, msem, ysem, hss, hrs, ess, ers, as_, ar_, bs_, br_, cs_, cr_, ds_, dr_,
+    gl, ra, gb, gf,
+    osem, msem, ysem, hss, hrs, ess, ers, as_, ar_, bs_, br_, cs_, cr_,
 ):
     dx = lax.axis_index("dx")
     dy = lax.axis_index("dy")
@@ -279,41 +279,32 @@
             grams += [total[:, 0:128] + (total[:, 128:] + cross), block]
     keep = pltpu.make_async_copy(both, yout, ysem)
     keep.start()
-    gl[...] = jnp.concatenate(grams, axis=0).reshape(8, 48, 128)
-
+    gl[...] = jnp.concatenate(grams, axis=0).reshape(16, 24, 128)
+
+    copies = []
+    for d in range(1, ndy):
+        peer = lax.rem(dy + d, ndy)
+        copies.append(remote(gl.at[peer], ra.at[dy], as_.at[d], ar_.at[d], (dx, peer)))
+    for copy in copies:
+        copy.wait()
+    chunk = gl[dy]
+    for d in range(1, ndy):
+        chunk += ra[lax.rem(dy + d, ndy)]
+    gb[dx] = chunk
     copies = []
     for d in range(1, ndx):
         peer = lax.rem(dx + d, ndx)
-        copies.append(remote(gl.at[peer], ra.at[dx], as_.at[d], ar_.at[d], (peer, dy)))
+        copies.append(remote(gb.at[dx], gb.at[dx], bs_.at[d], br_.at[d], (peer, dy)))
     for copy in copies:
         copy.wait()
-    chunk = gl[dx]
-    for d in range(1, ndx):
-        chunk += ra[lax.rem(dx + d, ndx)]
-    for p in range(16):
-        sb[p] = chunk[3 * p : 3 * p + 3]
+    chunk = gb[0]
+    for p in range(1, ndx):
+        chunk += gb[p]
+    gf[dy] = chunk
     copies = []
     for d in range(1, ndy):
         peer = lax.rem(dy + d, ndy)
-        copies.append(remote(sb.at[peer], rb.at[dy], bs_.at[d], br_.at[d], (dx, peer)))
-    for copy in copies:
-        copy.wait()
-    piece = sb[dy]
-    for d in range(1, ndy):
-        piece += rb[lax.rem(dy + d, ndy)]
-    gb[dy] = piece
-    copies = []
-    for d in range(1, ndy):
-        peer = lax.rem(dy + d, ndy)
-        copies.append(remote(gb.at[dy], gb.at[dy], cs_.at[d], cr_.at[d], (dx, peer)))
-    for copy in copies:
-        copy.wait()
-    for p in range(16):
-        gf[dx, 3 * p : 3 * p + 3] = gb[p]
-    copies = []
-    for d in range(1, ndx):
-        peer = lax.rem(dx + d, ndx)
-        copies.append(remote(gf.at[dx], gf.at[dx], ds_.at[d], dr_.at[d], (peer, dy)))
+        copies.append(remote(gf.at[dy], gf.at[dy], cs_.at[d], cr_.at[d], (dx, peer)))
     for copy in copies:
         copy.wait()
     grams = gf[...].reshape(384, 128)
@@ -481,12 +472,10 @@
                 pltpu.VMEM((2, 2, 195, 128), BF16),
                 pltpu.VMEM((3, 2, 195, 128), BF16),
                 pltpu.VMEM((3, 4, 2, 13, 128), BF16),
-                pltpu.VMEM((8, 48, 128), F32),
-                pltpu.VMEM((8, 48, 128), F32),
-                pltpu.VMEM((16, 3, 128), F32),
-                pltpu.VMEM((16, 3, 128), F32),
-                pltpu.VMEM((16, 3, 128), F32),
-                pltpu.VMEM((8, 48, 128), F32),
+                pltpu.VMEM((16, 24, 128), F32),
+                pltpu.VMEM((16, 24, 128), F32),
+                pltpu.VMEM((8, 24, 128), F32),
+                pltpu.VMEM((16, 24, 128), F32),
                 dma,
                 dma((8,)),
                 dma,
@@ -494,14 +483,12 @@
                 dma((2, 3)),
                 dma((3, 2, 8)),
                 dma((3, 2, 8)),
+                dma((16,)),
+                dma((16,)),
                 dma((8,)),
                 dma((8,)),
                 dma((16,)),
                 dma((16,)),
-                dma((16,)),
-                dma((16,)),
-                dma((8,)),
-                dma((8,)),
             ],
             compiler_params=pltpu.CompilerParams(collective_id=0, has_side_effects=True),
             name="filter",

time: 65.2 us -> 62.1 us (0.952)
  Pallas kernels: 64.8 us -> 61.7 us
    pallas_call x1, Pallas kernels: 54.7 us -> 51.6 us  [shards(): pl.pallas_call(lambda *refs: filter_kernel(ndx, ndy, *refs), out_shape=(j...]
where the time goes in v7:
time: 62.1 us; the launch traced here: 61.9 us
  Pallas kernels  61.7 us (99%)
    pallas_call x1, Pallas kernels, shards(): pl.pallas_call(lambda *refs: filter_kernel(ndx, ndy, *refs), out_shape=(j...  51.6 us
    pallas_call x1, Pallas kernels, shards(): pl.pallas_call(lambda *refs: basis_kernel(scale, *refs), out_shape=jax.Sh...  10.1 us

profile of v7, /device:TPU:1, one launch (start us, length us, event | category | flops | bytes accessed | tf_op | source)
XLA Modules:
  0.0 61.9 jit_solution(8329418122147909127)
XLA Ops:
  0.0 51.6 %filter.1 = (bf16[2912,512]{1,0:T(8,128)(2,1)}, f32[256,256]{1,0:T(8,128)}) custom-call(bf16[14,13,14,256]{3,2,1,0:T(8,128)(2,1)} %bitcast.2, bf16[2,2,2,512,512]{4,3,2,1,0:T(8,128)(2,1)} %refs_1_.1, s32[2,2,2,512]{3,2,1,0:T(2,128)} %refs_2_.1), custom_call_target="tpu_custom_call" | custom-call | tf_op jit(solution)/shard_map/filter/pallas_call | solution.py:441
  51.6 10.1 %basis.1 = f32[14,13,14,256]{3,2,1,0:T(8,128)} custom-call(bf16[2912,512]{1,0:T(8,128)(2,1)} %get-tuple-element.7.refs_0_, f32[256,256]{1,0:T(8,128)} %get-tuple-element.8.refs_1_), custom_call_target="tpu_custom_call" | custom-call | tf_op jit(solution)/shard_map/basis/pallas_call | solution.py:496

commit v8 on v7

--- a/solution.py
+++ b/solution.py
@@ -33,12 +33,12 @@
 
 def filter_kernel(
     ndx, ndy,
-    orb, mats, conn,
+    orb, mats, links_in,
     yout, gout,
-    obuf, abuf, ap, rmap, st, tt, ya2, yb2, acc2, both,
+    obuf, conn, abuf, ap, rmap, st, tt, ya2, yb2, acc2, both, rim, edge, gram,
     hx, hy, hc, shy, shc, sxl, sxh, syl, syh, scs, rxl, rxh, ryl, ryh, rcs,
     gl, ra, gb, gf,
-    osem, msem, ysem, hss, hrs, ess, ers, as_, ar_, bs_, br_, cs_, cr_,
+    osem, csem, msem, ysem, hss, hrs, ess, ers, as_, ar_, bs_, br_, cs_, cr_,
 ):
     dx = lax.axis_index("dx")
     dy = lax.axis_index("dy")
@@ -55,6 +55,8 @@
 
     first_load = pltpu.make_async_copy(orb, obuf, osem)
     first_load.start()
+    link_load = pltpu.make_async_copy(links_in, conn, csem)
+    link_load.start()
     loads = []
     for e in range(8):
         copy = pltpu.make_async_copy(mats.at[e // 4, e // 2 % 2, e % 2], abuf.at[e], msem.at[e])
@@ -124,19 +126,28 @@
         def _():
             copy.start()
 
-        return copy, ahead, behind
+        return copy, (sx, sy), ahead, behind
+
+    sent = {}
 
     def wait(copies):
-        for copy, ahead, behind in copies:
+        for copy, side, ahead, behind in copies:
 
             @pl.when(behind)
             def _():
                 copy.wait_recv()
 
+            sent.setdefault(side, (ahead, []))[1].append(copy)
+
+    def drain():
+        for ahead, copies in sent.values():
+
             @pl.when(ahead)
             def _():
-                copy.wait_send()
-
+                for copy in copies:
+                    copy.wait_send()
+
+    link_load.wait()
     fold(0)
     pl.semaphore_wait(barrier, len(partners))
     halo = []
@@ -221,8 +232,8 @@
             bump(14, 15, 1, gated(x_high, rcs[t, 2, h], coef))
             bump(0, 13, 1, gated(y_high, rcs[t, 3, h], coef))
             y[h, 0] = jnp.where(x_low, y[h, 0], 0.0)
-            edge = y2[h, line(0, 15, 15), :]
-            y2[h, line(0, 15, 15), :] = jnp.where(y_low, edge, 0.0)
+            kept = jnp.where(y_low, y2[h, line(0, 15, 15), :], 0.0)
+            y2[h, line(0, 15, 15), :] = kept
 
     stages = []
     for h in range(2):
@@ -251,40 +262,47 @@
     for h in range(2):
         yb2[h] = 0.5 * acc2[h] - 0.75 * ya2[h] - yb2[h]
 
-    def pair(h):
-        high = both[:, 128 * h : 128 * h + 128]
-        low = both[:, NB + 128 * h : NB + 128 * h + 128]
-        return high, low, jnp.concatenate([high, low], axis=1)
-
-    def diagonal(h):
-        high, _, pairs = pair(h)
-        total = dot_tn(high, pairs)
-        cross = total[:, 128:]
-        return total[:, 0:128] + (cross + cross.T)
-
+    def parts(y):
+        top = y.astype(BF16)
+        return top, (y - top.astype(F32)).astype(BF16)
+
+    def gram_of(ref):
+        total = dot_tn(ref[:, 0:NB], ref[...])
+        cross = total[:, NB:]
+        return total[:, 0:NB] + (cross + cross.T)
+
+    slot = lax.broadcasted_iota(jnp.int32, (169, 16, 128), 1)
+    for h in range(2):
+        inner = jnp.where(slot < 13, yb[h, 1:14].reshape(169, 16, 128), 0.0).reshape(2704, 128)
+        top, low = parts(inner)
+        both[0:2704, 128 * h : 128 * h + 128] = top
+        both[0:2704, NB + 128 * h : NB + 128 * h + 128] = low
+        rim[h, 368:384, :] = jnp.zeros((16, 128), F32)
+    gram[...] = gram_of(both.at[0:2704])
     for h in range(2):
         wait(stages[h])
         faces(2, h, yb, yb2, 0.5)
         yb2[h, line(0, 15, 15), :] = jnp.zeros((195, 128), F32)
-        y = yb2[h, 208:3120, :]
-        top = y.astype(BF16)
-        both[:, 128 * h : 128 * h + 128] = top
-        both[:, NB + 128 * h : NB + 128 * h + 128] = (y - top.astype(F32)).astype(BF16)
-        block = diagonal(h)
-        if h == 0:
-            grams = [block]
-        else:
-            total = dot_tn(both[:, 0:128], pair(1)[2])
-            cross = dot_tn(both[:, NB : NB + 128], both[:, 128:NB])
-            grams += [total[:, 0:128] + (total[:, 128:] + cross), block]
-    keep = pltpu.make_async_copy(both, yout, ysem)
-    keep.start()
-    gl[...] = jnp.concatenate(grams, axis=0).reshape(16, 24, 128)
+        rim[h, 0:208, :] = yb2[h, 2912:3120, :]
+        rim[h, 208:377, :] = yb2[h, line(1, 13, 13), :]
+        top, low = parts(rim[h])
+        edge[:, 128 * h : 128 * h + 128] = top
+        edge[:, NB + 128 * h : NB + 128 * h + 128] = low
+    full = gram[...] + gram_of(edge)
+    blocks = [full[0:128, 0:128], full[0:128, 128:NB], full[128:NB, 128:NB]]
+    gl[...] = jnp.concatenate(blocks, axis=0).reshape(16, 24, 128)
 
     copies = []
     for d in range(1, ndy):
         peer = lax.rem(dy + d, ndy)
         copies.append(remote(gl.at[peer], ra.at[dy], as_.at[d], ar_.at[d], (dx, peer)))
+    for h in range(2):
+        top, low = parts(yb2[h, 208:3120, :])
+        both[:, 128 * h : 128 * h + 128] = top
+        both[:, NB + 128 * h : NB + 128 * h + 128] = low
+    keep = pltpu.make_async_copy(both, yout, ysem)
+    keep.start()
+    drain()
     for copy in copies:
         copy.wait()
     chunk = gl[dy]
@@ -444,10 +462,11 @@
                 jax.ShapeDtypeStruct((2912, 2 * NB), BF16),
                 jax.ShapeDtypeStruct((NB, NB), F32),
             ),
-            in_specs=[anywhere, anywhere, vmem],
+            in_specs=[anywhere, anywhere, anywhere],
             out_specs=(anywhere, vmem),
             scratch_shapes=[
                 pltpu.VMEM((14, 13, 14, NB), BF16),
+                pltpu.VMEM((2, 2, 2, 512), jnp.int32),
                 pltpu.VMEM((8, 512, 512), BF16),
                 pltpu.VMEM((8, 448, 448), BF16),
                 pltpu.VMEM((2, 448, 128), jnp.int32),
@@ -457,6 +476,9 @@
                 pltpu.VMEM((2, 3120, 128), F32),
                 pltpu.VMEM((2, 3120, 128), F32),
                 pltpu.VMEM((2912, 2 * NB), BF16),
+                pltpu.VMEM((2, 384, 128), F32),
+                pltpu.VMEM((384, 2 * NB), BF16),
+                pltpu.VMEM((NB, NB), F32),
                 pltpu.VMEM((2, 13, 14, 128), BF16),
                 pltpu.VMEM((2, 182, 128), BF16),
                 pltpu.VMEM((2, 13, 128), BF16),
@@ -476,6 +498,7 @@
                 pltpu.VMEM((16, 24, 128), F32),
                 pltpu.VMEM((8, 24, 128), F32),
                 pltpu.VMEM((16, 24, 128), F32),
+                dma,
                 dma,
                 dma((8,)),
                 dma,

time: 62.1 us -> 60.4 us (0.973)
  Pallas kernels: 61.7 us -> 60.1 us
    pallas_call x1, Pallas kernels: 51.6 us -> 50 us  [shards(): pl.pallas_call(lambda *refs: filter_kernel(ndx, ndy, *refs), out_shape=(j...]
where the time goes in v8:
time: 60.4 us; the launch traced here: 60.3 us
  Pallas kernels  60.1 us (100%)
    pallas_call x1, Pallas kernels, shards(): pl.pallas_call(lambda *refs: filter_kernel(ndx, ndy, *refs), out_shape=(j...  50 us
    pallas_call x1, Pallas kernels, shards(): pl.pallas_call(lambda *refs: basis_kernel(scale, *refs), out_shape=jax.Sh...  10.1 us

profile of v8, /device:TPU:1, one launch (start us, length us, event | category | flops | bytes accessed | tf_op | source)
XLA Modules:
  0.0 60.3 jit_solution(7484370037342599463)
XLA Ops:
  0.0 50.0 %filter.1 = (bf16[2912,512]{1,0:T(8,128)(2,1)}, f32[256,256]{1,0:T(8,128)}) custom-call(bf16[14,13,14,256]{3,2,1,0:T(8,128)(2,1)} %bitcast.2, bf16[2,2,2,512,512]{4,3,2,1,0:T(8,128)(2,1)} %refs_1_.1, s32[2,2,2,512]{3,2,1,0:T(2,128)} %refs_2_.1), custom_call_target="tpu_custom_call" | custom-call | tf_op jit(solution)/shard_map/filter/pallas_call | solution.py:459
  50.0 10.1 %basis.1 = f32[14,13,14,256]{3,2,1,0:T(8,128)} custom-call(bf16[2912,512]{1,0:T(8,128)(2,1)} %get-tuple-element.7.refs_0_, f32[256,256]{1,0:T(8,128)} %get-tuple-element.8.refs_1_), custom_call_target="tpu_custom_call" | custom-call | tf_op jit(solution)/shard_map/basis/pallas_call | solution.py:519

commit v9 on v8

--- a/solution.py
+++ b/solution.py
@@ -197,19 +197,19 @@
 
         corners = [(0, 15, -1, -1), (14, 13, 1, 1), (0, 13, -1, 1), (14, 15, 1, -1)]
         count = 4 if t < 2 else 1
-        for n, (i, slot, _, _) in enumerate(corners[:count]):
+        for n, (i, slot, sx, sy) in enumerate(corners[:count]):
             scs[t, n, h] = acc2[h, line(i, slot, 1), :].astype(BF16)
+        for n, (_, _, sx, sy) in enumerate(corners[:count]):
+            send(4 + n, scs.at[t, n, h], rcs.at[t, n, h], sx, sy)
         syl[t, h] = acc2[h, line(0, 15, 15), :].astype(BF16)
         if t < 2:
             syh[t, h] = acc2[h, line(0, 13, 15), :].astype(BF16)
+        send(0, syl.at[t, h], ryh.at[t, h], 0, -1)
+        if t < 2:
+            send(1, syh.at[t, h], ryl.at[t, h], 0, 1)
         sxl[t, h] = acc[h, 0].astype(BF16)
         if t < 2:
             sxh[t, h] = acc[h, 14].astype(BF16)
-        for n, (_, _, sx, sy) in enumerate(corners[:count]):
-            send(4 + n, scs.at[t, n, h], rcs.at[t, n, h], sx, sy)
-        send(0, syl.at[t, h], ryh.at[t, h], 0, -1)
-        if t < 2:
-            send(1, syh.at[t, h], ryl.at[t, h], 0, 1)
         send(2, sxl.at[t, h], rxh.at[t, h], -1, 0)
         if t < 2:
             send(3, sxh.at[t, h], rxl.at[t, h], 1, 0)
@@ -292,6 +292,7 @@
     blocks = [full[0:128, 0:128], full[0:128, 128:NB], full[128:NB, 128:NB]]
     gl[...] = jnp.concatenate(blocks, axis=0).reshape(16, 24, 128)
 
+    pending = []
     copies = []
     for d in range(1, ndy):
         peer = lax.rem(dy + d, ndy)
@@ -304,7 +305,8 @@
     keep.start()
     drain()
     for copy in copies:
-        copy.wait()
+        copy.wait_recv()
+    pending += copies
     chunk = gl[dy]
     for d in range(1, ndy):
         chunk += ra[lax.rem(dy + d, ndy)]
@@ -314,7 +316,8 @@
         peer = lax.rem(dx + d, ndx)
         copies.append(remote(gb.at[dx], gb.at[dx], bs_.at[d], br_.at[d], (peer, dy)))
     for copy in copies:
-        copy.wait()
+        copy.wait_recv()
+    pending += copies
     chunk = gb[0]
     for p in range(1, ndx):
         chunk += gb[p]
@@ -324,12 +327,15 @@
         peer = lax.rem(dy + d, ndy)
         copies.append(remote(gf.at[dy], gf.at[dy], cs_.at[d], cr_.at[d], (dx, peer)))
     for copy in copies:
-        copy.wait()
+        copy.wait_recv()
+    pending += copies
     grams = gf[...].reshape(384, 128)
     gout[0:128, 0:128] = grams[0:128]
     gout[0:128, 128:NB] = grams[128:NB]
     gout[128:NB, 0:128] = jnp.zeros((128, 128), F32)
     gout[128:NB, 128:NB] = grams[NB:384]
+    for copy in pending:
+        copy.wait_send()
     keep.wait()
 
 
@@ -435,7 +441,7 @@
     weights[2 * NB :] = (w - top.astype(F32)).astype(BF16)
     load.wait()
     copies = []
-    for start, count in ((0, 4), (4, 4), (8, 4), (12, 2)):
+    for start, count in ((0, 2), (2, 4), (6, 4), (10, 3), (13, 1)):
         rows = slice(208 * start, 208 * (start + count))
         left = jnp.concatenate([ybuf[rows, :], ybuf[rows, 0:NB]], axis=1)
         q = dot_nn(left, weights[...]).reshape(count, 13, 16, NB)

time: 60.4 us -> 60.5 us (level)
  no operation moved by 1% of the time
where the time goes in v9:
time: 60.5 us; the launch traced here: 60.4 us
  Pallas kernels  60.2 us (100%)
    pallas_call x1, Pallas kernels, shards(): pl.pallas_call(lambda *refs: filter_kernel(ndx, ndy, *refs), out_shape=(j...  50.1 us
    pallas_call x1, Pallas kernels, shards(): pl.pallas_call(lambda *refs: basis_kernel(scale, *refs), out_shape=jax.Sh...  10.1 us

profile of v9, /device:TPU:1, one launch (start us, length us, event | category | flops | bytes accessed | tf_op | source)
XLA Modules:
  0.0 60.4 jit_solution(15473364806541572538)
XLA Ops:
  0.0 50.1 %filter.1 = (bf16[2912,512]{1,0:T(8,128)(2,1)}, f32[256,256]{1,0:T(8,128)}) custom-call(bf16[14,13,14,256]{3,2,1,0:T(8,128)(2,1)} %bitcast.2, bf16[2,2,2,512,512]{4,3,2,1,0:T(8,128)(2,1)} %refs_1_.1, s32[2,2,2,512]{3,2,1,0:T(2,128)} %refs_2_.1), custom_call_target="tpu_custom_call" | custom-call | tf_op jit(solution)/shard_map/filter/pallas_call | solution.py:465
  50.1 10.1 %basis.1 = f32[14,13,14,256]{3,2,1,0:T(8,128)} custom-call(bf16[2912,512]{1,0:T(8,128)(2,1)} %get-tuple-element.7.refs_0_, f32[256,256]{1,0:T(8,128)} %get-tuple-element.8.refs_1_), custom_call_target="tpu_custom_call" | custom-call | tf_op jit(solution)/shard_map/basis/pallas_call | solution.py:525
